TPU v7x, 256 devices: a whole 4x4x8 slice. The times are simulated.
256 devices in a mesh: dp: 8 (over x, core), ctx: 32 (over z, y).
Axes of the slice: x: 4, y: 4, z: 8, core: 2. Of those that a mesh axis runs over, the one named last changes fastest.
Arguments:
- tokens: bfloat16 [8, 4096, 4096], P('dp', 'ctx'), may hold values from -6 to 6
- qk_weight: bfloat16 [4096, 512], replicated, may hold values from -0.09375 to 0.09375
- conv_weight: float32 [3, 512], replicated, may hold values from -3 to 3
- values: bfloat16 [8, 4096, 2048], P('dp', 'ctx'), may hold values from -6 to 6
- cotangent: bfloat16 [8, 4096, 2048], P('dp', 'ctx'), may hold values from -6 to 6
Outputs:
- mixed_out: bfloat16 [8, 4096, 2048], P('dp', 'ctx')
- grad_tokens: bfloat16 [8, 4096, 4096], P('dp', 'ctx')
- grad_values: bfloat16 [8, 4096, 2048], P('dp', 'ctx')
- grad_qk_weight: float32 [4096, 512], P('ctx')
All inputs are finite; a program needn't handle non-finite values.
Results may differ from a plain program's by a relative error of at most 0.04.
Values sent between devices are 32-bit elements; how exact they have to be, the bound alone decides.
No kernel may reach another device: no remote copies, remote signals or barrier semaphores. Data moves between devices by JAX's collectives and lax.ppermute only.
A program may use at most 128 MiB of HBM per device.

v0:
```python
import jax
import jax.numpy as jnp
import numpy as np
from jax import lax
from jax.experimental import pallas as pl
from jax.experimental.pallas import tpu as pltpu
from jax.sharding import Mesh, PartitionSpec as P

H = 16
F = 16
V = 128
NX, NC, NZ, NY = 4, 2, 8, 4
T = 128
TS = T * NY
HG = H // NY
E = 160
EP = 256
f32 = jnp.float32
bf16 = jnp.bfloat16


def feature_tables():
    first = np.zeros((128, 512), np.float32)
    weight = np.zeros((8, EP), np.float32)
    for f in range(128):
        i, d = f % 16, f // 16
        first[i, f] = 1
        first[(i + d) % 16, 128 + f] = 1
        weight[:, f] = 1 / 32 if d == 0 else 1 / 16
    for f in range(8):
        first[f, 256 + f] = 1
        first[f + 8, 384 + f] = 1
        weight[:, 128 + f] = 1 / 16
    for f in range(16):
        first[f, 256 + 8 + f] = 1
        first[16, 384 + 8 + f] = 0.5
        weight[:, 128 + 8 + f] = 1 / 4
    first[16, 256 + 24] = 0.5
    first[16, 384 + 24] = 0.5
    weight[:, 128 + 24] = 1
    sel_q = first.copy()
    sel_q[64:80] = first[:16]
    sel_k = first.copy()
    sel_k[32:48] = first[:16]
    return sel_q, sel_k, weight


SEL_Q, SEL_K, WEIGHT = feature_tables()
BIT_REVERSED = (0, 4, 2, 6, 1, 5, 3, 7)


def mm(a, b):
    return lax.dot_general(a, b, (((1,), (0,)), ((), ())), preferred_element_type=f32)


def mm_nt(a, b):
    return lax.dot_general(a, b, (((1,), (1,)), ((), ())), preferred_element_type=f32)


def mm_tn(a, b):
    return lax.dot_general(a, b, (((0,), (0,)), ((), ())), preferred_element_type=f32)


def run(kernel, outs, *args, scratch=(), smem=0, us=0.5):
    vm = pl.BlockSpec(memory_space=pltpu.VMEM)
    sm = pl.BlockSpec(memory_space=pltpu.SMEM)
    return pl.pallas_call(
        kernel,
        out_shape=[jax.ShapeDtypeStruct(s, d) for s, d in outs],
        in_specs=[sm] * smem + [vm] * (len(args) - smem),
        out_specs=[vm] * len(outs),
        scratch_shapes=list(scratch),
        compiler_params=pltpu.CompilerParams(vmem_limit_bytes=12 << 20),
        cost_estimate=pl.CostEstimate(
            flops=0, bytes_accessed=int(us * 3.5e6), transcendentals=0
        ),
    )(*args)


def timed(us, *args, **kwargs):
    return run(*args, us=us, **kwargs)


def features(u, sel):
    x = mm(u, sel)
    return jnp.concatenate([x[:, :128] * x[:, 128:256], x[:, 256:384] * x[:, 384:]], 1)


def feature_grad(u, sel, grad):
    x = mm(u, sel)
    g1, g2 = grad[:, :128], grad[:, 128:]
    stacked = jnp.concatenate(
        [g1 * x[:, 128:256], g1 * x[:, :128], g2 * x[:, 384:], g2 * x[:, 256:384]], 1
    ).astype(bf16)
    return mm_nt(stacked, sel)


def causal(rows, r):
    row = lax.broadcasted_iota(jnp.int32, (T, rows), 0) + r * T
    col = lax.broadcasted_iota(jnp.int32, (T, rows), 1)
    return row >= col


def lanes(h):
    return pl.ds(pl.multiple_of(h * V, V), V)


def turned(y, s):
    return lax.rem(y[0] + (s + NY), NY)


def group_lanes(g, width):
    return pl.ds(pl.multiple_of(g * width, width), width)


def pack_kernel(y, a, *outs):
    for s, o in enumerate(outs):
        o[...] = a[:, group_lanes(turned(y, s), HG * V)].astype(f32)


def after(value, *others):
    return lax.optimization_barrier((value, *others))[0]


def pack_columns_kernel(y, a, *outs):
    for s, o in enumerate(outs):
        for k in range(NZ):
            o[:, k * T : (k + 1) * T] = a[:, group_lanes(turned(y, s) + k * NY, T)].astype(f32)


def flip_kernel(y, a0, a1, a2, a3, flipped):
    for s, a in enumerate((a0, a1, a2, a3)):
        cols = group_lanes(turned(y, -s), T)
        for k in range(NZ):
            t = jnp.transpose(a[:, k * T : (k + 1) * T]).astype(bf16)
            for part in range(NC * NX):
                at = part * T + BIT_REVERSED[k] * 16
                flipped[at : at + 16, cols] = t[part * 16 : part * 16 + 16]


def mix_kernel(y, projected, halo, cw, o0, o1, o2, o3, pad, blocks):
    pad[:8] = halo[...]
    pad[8:] = projected[...]
    m = projected[...] * cw[0:1]
    for j in (1, 2):
        m += pad[8 - j : 8 - j + T] * cw[j : j + 1]
    lane = lax.broadcasted_iota(jnp.int32, (T, 128), 1)
    for g in range(NY):
        at = (g // 2) * 128
        q, k = m[:, at : at + 128], m[:, 256 + at : 256 + at + 128]
        if g % 2:
            q = pltpu.roll(q, 64, 1)
        else:
            k = pltpu.roll(k, 64, 1)
        blocks[g] = jnp.where(lane < 64, q, k)
    for s, o in enumerate((o0, o1, o2, o3)):
        o[...] = blocks[turned(y, s)]


def prepare_kernel(y, b0, b1, b2, b3, sel_k, w, uq, uk, tot, mg):
    for s, b in enumerate((b0, b1, b2, b3)):
        mg[group_lanes(turned(y, -s), T)] = b[...]
    lane = lax.broadcasted_iota(jnp.int32, (TS, 128), 1)
    tot[...] = jnp.zeros_like(tot)

    def one(h, _):
        for is_key in (0, 1):
            x = pltpu.roll(mg[...], (256 - 64 * is_key) - 16 * h, 1)
            hi = x.astype(bf16).astype(f32)
            lo = x - hi
            a, b = (lo, hi) if is_key else (hi, lo)
            u = jnp.where(lane < 16, hi, jnp.where(lane == 16, 2.0, 0.0))
            u = jnp.where((lane >= 32) & (lane < 48), pltpu.roll(a, 32, 1), u)
            u = jnp.where((lane >= 64) & (lane < 80), pltpu.roll(b, 64, 1), u)
            (uk if is_key else uq)[h] = u.astype(bf16)
        rk = features(uk[h], sel_k[...])
        tot[pl.ds(h, 1)] = jnp.sum(rk, 0, keepdims=True) * w[0:1]
        return 0

    lax.fori_loop(0, HG, one, 0)


def halves(scratch, p, keep, send):
    keep[...] = scratch[p]
    send[...] = scratch[1 - p]


def state_kernel(p, y, uq, uk, v0, v1, v2, v3, sel_k, w, keep, send, vb, rs, scratch):
    for s, v in enumerate((v0, v1, v2, v3)):
        vb[group_lanes(turned(y, -s), T)] = v[...].astype(bf16)

    def one(h, _):
        rk = (features(uk[h], sel_k[...]) * w[0:1]).astype(bf16)
        s = mm_tn(rk, vb[:, lanes(h)])
        scratch[lax.div(h, 2), pl.ds(pl.multiple_of(lax.rem(h, 2) * E, E), E)] = s[:E]
        for r in range(NY):
            rows = (r + 1) * T
            t = mm_nt(uq[h, r * T : rows], uk[h, :rows])
            t = jnp.where(causal(rows, r), 0.5 + t * t * (1 / 32), 0.0)
            rs[h, r * T : rows] = jnp.broadcast_to(jnp.sum(t, 1, keepdims=True), (T, V))
        return 0

    lax.fori_loop(0, HG, one, 0)
    halves(scratch, p[0], keep, send)


def denom_kernel(p, y, uq, rs, etot, c0, c1, c2, c3, sel_q, w, keep, send, dn, inv, scratch):
    def one(h, _):
        rq = features(uq[h], sel_q[...])
        den = rs[h] + jnp.sum(rq * etot[pl.ds(h, 1)], 1, keepdims=True)
        iv = 1.0 / den
        inv[h] = iv
        for s, c in enumerate((c0, c1, c2, c3)):
            rows = group_lanes(turned(y, -s), T)
            dn[rows, lanes(h)] = (c[:, lanes(h)] * inv[h, rows]).astype(bf16)
        s = mm_tn((rq * w[0:1]).astype(bf16), dn[:, lanes(h)])
        scratch[lax.div(h, 2), pl.ds(pl.multiple_of(lax.rem(h, 2) * E, E), E)] = s[:E]
        return 0

    lax.fori_loop(0, HG, one, 0)
    halves(scratch, p[0], keep, send)


def pair_kernel(use, keep, got, e0, e1, e2, own, partner):
    base = e0[...] + e1[...] + e2[...]
    own[...] = base + jnp.where(use[0] > 0, got[...], 0.0)
    partner[...] = base + jnp.where(use[0] > 0, 0.0, keep[...])


def fill_states(p, own, got, scratch):
    zero = jnp.zeros((EP - E, V), bf16)
    for which, a in ((p, own), (1 - p, got)):
        for i in range(2):
            scratch[2 * which + i, :E] = a[i * E : (i + 1) * E].astype(bf16)
            scratch[2 * which + i, E:] = zero


def local_kernel(
    p, y, uq, uk, vb, dn, inv, etot, own, got, sel_q, w,
    o0, o1, o2, o3, dq, gv, dk, gtot, dk_acc, states, out,
):
    lane = lax.broadcasted_iota(jnp.int32, (TS, 128), 1)
    gtot[...] = jnp.zeros_like(gtot)
    dq[...] = jnp.zeros_like(dq)
    dk[...] = jnp.zeros_like(dk)
    fill_states(p[0], own, got, states)

    def one(h, _):
        cols = lanes(h)
        c = states[h]
        tot_row = etot[pl.ds(h, 1)]
        gsum = jnp.zeros((1, EP), f32)
        grads = []
        for r in reversed(range(NY)):
            rows = (r + 1) * T
            mine = slice(r * T, rows)
            u = uq[h, mine]
            keep = causal(rows, r)
            s = mm_nt(u, uk[h, :rows])
            pr = jnp.where(keep, 0.5 + s * s * (1 / 32), 0.0).astype(bf16)
            rq = features(u, sel_q[...])
            numer = mm(pr, vb[:rows, cols]) + mm(rq.astype(bf16), c)
            o = numer * inv[h, mine]
            out[r, :, cols] = o
            d = dn[mine, cols]
            dd = -jnp.sum(d.astype(f32) * o, 1, keepdims=True)
            dp = mm_nt(d, vb[:rows, cols]) + dd
            ds = jnp.where(keep, dp * s * (1 / 16), 0.0).astype(bf16)
            gsum += jnp.sum(rq * dd, 0, keepdims=True)
            dr = mm_nt(d, c) + dd * tot_row
            grads.append(mm(ds, uk[h, :rows]) + feature_grad(u, sel_q[...], dr))
            gv_add = mm_tn(pr, d)
            dk_add = mm_tn(ds, u)
            if r == NY - 1:
                gv[:, cols] = gv_add
                dk_acc[...] = dk_add
            else:
                gv[:rows, cols] += gv_add
                dk_acc[:rows] += dk_add
        gtot[pl.ds(h, 1)] = gsum * w[0:1]
        g = jnp.concatenate(grads[::-1], 0)
        dq[...] += pltpu.roll(jnp.where(lane < 16, g, 0.0), 16 * h, 1)
        dk[...] += pltpu.roll(jnp.where(lane < 16, dk_acc[...], 0.0), 64 + 16 * h, 1)
        return 0

    lax.fori_loop(0, HG, one, 0)
    for s, o in enumerate((o0, o1, o2, o3)):
        o[...] = out[turned(y, s)]


def key_kernel(
    p, y, uk, vb, gv_in, dq, dk, own, got, egtot, sel_k,
    o0, o1, o2, o3, gm, edge, states, gv,
):
    lane = lax.broadcasted_iota(jnp.int32, (TS, 128), 1)
    fill_states(p[0], own, got, states)
    gm[...] = dq[...] + dk[...]

    def one(h, _):
        cols = lanes(h)
        c = states[h]
        rk = features(uk[h], sel_k[...]).astype(bf16)
        gv[:, cols] = gv_in[:, cols] + mm(rk, c)
        dr = mm_nt(vb[:, cols], c) + egtot[pl.ds(h, 1)]
        g = feature_grad(uk[h], sel_k[...], dr)
        gm[...] += pltpu.roll(jnp.where(lane < 16, g, 0.0), 64 + 16 * h, 1)
        return 0

    lax.fori_loop(0, HG, one, 0)
    edge[...] = gm[:8]
    for s, o in enumerate((o0, o1, o2, o3)):
        o[...] = gv[group_lanes(turned(y, s), T)]


def conv_back_kernel(y, gm, halo, cw, gp, pad):
    pad[:TS] = gm[...]
    pad[TS:] = halo[...]
    cols = group_lanes(y[0], 128)
    total = gm[...] * cw[0:1, cols]
    for j in (1, 2):
        total += pad[j : TS + j] * cw[j : j + 1, cols]
    gp[...] = total


def weight_kernel(at, g0, g1, g2, g3, flipped, keep, send, grad_own, gp):
    y, core = at[0], at[1]
    for s, g in enumerate((g0, g1, g2, g3)):
        gp[:, group_lanes(turned(at, -s), 128)] = g[...].astype(bf16)
    half = NZ * T // 2
    for which, ref in ((1 - core, send), (core, keep)):
        ref[...] = mm(flipped[group_lanes(which, half)], gp[...])
    grad_own[...] = gp[group_lanes(y, T)]


def split_x_kernel(x, a, b, o0, o1, o2, o3):
    for s, o in enumerate((o0, o1, o2, o3)):
        rows = pl.ds(pl.multiple_of(lax.rem(x[0] + s, NX) * T, T), T)
        o[...] = a[rows] + b[rows]


def split_z_kernel(bit, *refs):
    ins, (keep, send) = refs[:-2], refs[-2:]
    n = keep.shape[0]
    for which, o in ((bit[0], keep), (1 - bit[0], send)):
        rows = pl.ds(pl.multiple_of(which * n, n), n)
        total = ins[0][rows]
        for a in ins[1:]:
            total += a[rows]
        o[...] = total


def stack_kernel(core, a, b, c, d, o):
    total = a[...] + b[...]
    o[group_lanes(core[0], 16)] = total
    o[group_lanes(1 - core[0], 16)] = c[...] + d[...]


def finish_kernel(x, m0, m1, m2, m3, rows):
    lane = lax.broadcasted_iota(jnp.int32, (16, 128), 1)
    for s, m in enumerate((m0, m1, m2, m3)):
        src = lax.rem(x[0] - s + NX, NX)
        for core in range(NC):
            at = pl.ds(pl.multiple_of(core * 64 + src * 16, 16), 16)
            b = m[core * 16 : core * 16 + 16]
            for half in range(2):
                lo, hi = b[:, half * 256 : half * 256 + 128], b[:, half * 256 + 128 : half * 256 + 256]
                q = jnp.where(lane < 64, lo, pltpu.roll(hi, 64, 1))
                k = jnp.where(lane < 64, pltpu.roll(lo, 64, 1), hi)
                rows[at, half * 128 : half * 128 + 128] = q
                rows[at, 256 + half * 128 : 256 + half * 128 + 128] = k


def rows_kernel(y, b0, b1, b2, b3, rows):
    for s, b in enumerate((b0, b1, b2, b3)):
        rows[:, group_lanes(turned(y, -s), HG * V)] = b[...].astype(bf16)


def shift(value, axis, by):
    n = lax.axis_size(axis)
    return lax.ppermute(value, axis, [(i, (i + by) % n) for i in range(n)])


def shift_open(value, axis, by):
    n = lax.axis_size(axis)
    return lax.ppermute(
        value, axis, [(i, i + by) for i in range(n) if 0 <= i + by < n]
    )


def swap(value, axis, mask):
    n = lax.axis_size(axis)
    return lax.ppermute(value, axis, [(i, i ^ mask) for i in range(n)])


def totals_scan(tot, sign):
    near = sum(shift_open(tot, "z", sign * s) for s in (1, 2, 3))
    far = shift_open(near + tot, "z", sign * 4)
    return near + far


def across_pairs(keep, got, sign):
    total = keep + got
    return [shift_open(total, "z", sign * d) for d in (2, 4, 6)]


def back_to_pair(keep, got, others, use):
    half = ((2 * E, V), f32)
    own, partner = run(pair_kernel, [half, half], use, keep, got, *others, smem=1)
    return own, swap(partner, "z", 1)


def swap_y(blocks):
    return [blocks[0]] + [shift(blocks[s], "y", s) for s in (1, 2, 3)]


def on_device(tokens, qk_weight, conv_weight, values, cotangent):
    def place(name):
        return lax.axis_index(name).astype(jnp.int32)

    x, core, z, y = place("x"), place("core"), place("z"), place("y")
    y1, parity = y.reshape(1), lax.rem(z, 2).reshape(1)
    sel_q, sel_k = jnp.asarray(SEL_Q, bf16), jnp.asarray(SEL_K, bf16)
    w = jnp.asarray(WEIGHT, f32)
    local_x = tokens[0]
    wide = HG * V

    projected = jnp.dot(local_x, qk_weight, preferred_element_type=f32)
    halo = lax.ppermute(
        projected[T - 8 :], ("z", "y"), [(i, i + 1) for i in range(NZ * NY - 1)]
    )
    by_head = [((T, wide), f32)] * NY
    v_packed = run(pack_kernel, by_head, y1, after(values[0], projected), smem=1)
    c_packed = run(pack_kernel, by_head, y1, after(cotangent[0], projected), smem=1)
    mixed = run(
        mix_kernel, [((T, 128), f32)] * NY, y1, projected, halo, conv_weight, smem=1,
        scratch=[pltpu.VMEM((T + 8, 512), f32), pltpu.VMEM((NY, T, 128), f32)],
    )
    mixed = swap_y(mixed)
    v_all = swap_y(lax.optimization_barrier((*v_packed, *mixed))[:NY])
    uq, uk, tot = timed(
        2.6, prepare_kernel,
        [((HG, TS, 128), bf16), ((HG, TS, 128), bf16), ((8, EP), f32)],
        y1, *mixed, sel_k, w, smem=1, scratch=[pltpu.VMEM((TS, 128), f32)],
    )
    c_all = swap_y(lax.optimization_barrier((*c_packed, tot))[:NY])
    etot = totals_scan(tot, 1)
    half = ((2 * E, V), f32)
    half_scratch = [pltpu.VMEM((2, 2 * E, V), f32)]
    keep, send, vb, rs = timed(
        2.8, state_kernel, [half, half, ((TS, wide), bf16), ((HG, TS, V), f32)],
        parity, y1, uq, uk, *v_all, sel_k, w, smem=2, scratch=half_scratch,
    )
    g_keep, g_send, dn, inv = timed(
        2.4, denom_kernel, [half, half, ((TS, wide), bf16), ((HG, TS, V), f32)],
        parity, y1, uq, rs, etot, *c_all, sel_q, w, smem=2, scratch=half_scratch,
    )
    pair = swap(after(send, etot), "z", 1)
    g_pair = swap(g_send, "z", 1)
    earlier = across_pairs(keep, pair, 1)
    g_later = across_pairs(g_keep, g_pair, -1)
    own, got = back_to_pair(keep, after(pair, g_pair), earlier, parity)
    own = after(own, *g_later)
    g_own, g_got = back_to_pair(g_keep, g_pair, g_later, 1 - parity)

    x_packed = timed(
        1.5, pack_columns_kernel, [((T, NZ * T), f32)] * NY, y1, after(local_x, g_keep), smem=1
    )
    (flipped,) = timed(
        1.9, flip_kernel, [((NZ * T, TS), bf16)], y1, *swap_y(x_packed), smem=1
    )

    states = pltpu.VMEM((HG, EP, V), bf16)
    square = ((TS, 128), f32)
    *out, dq, gv_in, dk, gtot = timed(
        9.5, local_kernel,
        by_head + [square, ((TS, wide), f32), square, ((8, EP), f32)],
        parity, y1, uq, uk, vb, dn, inv, etot, own, got, sel_q, w, smem=2,
        scratch=[pltpu.VMEM((TS, 128), f32), states, pltpu.VMEM((NY, T, wide), f32)],
    )
    egtot = totals_scan(gtot, -1)

    def token_rows(blocks):
        return run(rows_kernel, [((T, H * V), bf16)], y1, *swap_y(blocks), smem=1)[0]

    mixed_out = token_rows(out)
    egtot = after(egtot, flipped)
    *gv, gm, edge = timed(
        3.5, key_kernel, by_head + [square, ((8, 128), f32)],
        parity, y1, uk, vb, gv_in, dq, dk, g_own, g_got, egtot, sel_k, smem=2,
        scratch=[states, pltpu.VMEM((TS, wide), f32)],
    )
    taps = conv_weight.shape[0]
    cw = jnp.transpose(conv_weight.reshape(taps, 2, NY, 64), (0, 2, 1, 3)).reshape(taps, 512)
    (gp,) = run(
        conv_back_kernel, [square], y1, after(gm, mixed_out), shift_open(edge, "z", -1), cw, smem=1,
        scratch=[pltpu.VMEM((TS + 8, 128), f32)],
    )
    blocks = [gp] + [shift(gp, "y", s) for s in (1, 2, 3)]
    keep, send, grad_own = timed(
        2.0, weight_kernel,
        [((NZ * T // 2, 512), f32), ((NZ * T // 2, 512), f32), ((T, 512), bf16)],
        jnp.stack([y, core]), *blocks, flipped, smem=1,
        scratch=[pltpu.VMEM((TS, 512), bf16)],
    )
    quarter = ((T, 512), f32)
    parts = run(
        split_x_kernel, [quarter] * NX, x.reshape(1), keep, swap(send, "core", 1), smem=1
    )
    own_rows = jnp.transpose(
        after(grad_own, parts[0]).reshape(T, NY, 2, 64), (0, 2, 1, 3)
    ).reshape(T, 512)
    grad_x = mm_nt(own_rows, qk_weight).astype(bf16)
    grad_values = token_rows(lax.optimization_barrier((*gv, parts[0]))[:NY])
    parts = [parts[0]] + [shift(parts[s], "x", s) for s in (1, 2, 3)]
    parts[0] = after(parts[0], grad_x, grad_values)
    for mask in (1, 2, 4):
        n = 64 // mask
        bit = lax.rem(lax.div(z, mask), 2).reshape(1)
        keep, send = run(
            split_z_kernel, [((n, 512), f32), ((n, 512), f32)], bit, *parts, smem=1
        )
        parts = [keep, swap(send, "z", mask)]
    (pair_rows,) = run(
        stack_kernel, [((32, 512), f32)], core.reshape(1), *parts,
        *[swap(a, "core", 1) for a in parts], smem=1,
    )
    stacks = [pair_rows] + [shift(pair_rows, "x", s) for s in (1, 2, 3)]
    (weight_grad,) = run(finish_kernel, [((T, 512), f32)], x.reshape(1), *stacks, smem=1)

    return (mixed_out[None], grad_x[None], grad_values[None], weight_grad)


def solution(mesh):
    inner = Mesh(mesh.devices.reshape(NX, NC, NZ, NY), ("x", "core", "z", "y"))
    rows = P(("x", "core"), ("z", "y"), None)
    return jax.shard_map(
        on_device,
        mesh=inner,
        in_specs=(rows, P(), P(), rows, rows),
        out_specs=(rows, rows, rows, P(("z", "y"), None)),
        check_vma=False,
    )
```

profile of v0, /device:TPU:8, one launch (start us, length us, event | category | flops | bytes accessed | tf_op | source)
XLA Modules:
  0.0 218.5 jit_solution(6794716458284529286)
XLA Ops:
  0.7 3.3 %fusion.projected = f32[128,512]{1,0:T(8,128)S(1)} fusion(bf16[4096,512]{1,0:T(8,128)(2,1)} %param.9, bf16[1,128,4096]{2,1,0:T(8,128)(2,1)} %param.8), kind=kOutput, calls=%fused_computation.5 | convolution fusion | flops 536870912 | bytes 5505024 | tf_op jit(solution)/shard_map/dot_general | solution.py:427
  4.0 3.6 %collective-permute-start = (f32[8,512]{1,0:T(8,128)S(1)}, f32[8,512]{1,0:T(8,128)S(1)}, u32[]{:S(2)}, u32[]{:S(2)}) collective-permute-start(f32[8,512]{1,0:T(8,128)S(1)} %slice.4), channel_id=1, source_target_pairs={{0,1},{1,2},{2,3},{3,4},{4,5},{5,6},{6,7},{7,8},{8,9},{9,10},{10,1... | collective-permute-start | bytes 49160 | tf_op jit(solution)/shard_map/ppermute | solution.py:428
  21.4 7.0 %collective-permute-start.9 = (f32[8,256]{1,0:T(8,128)S(1)}, f32[8,256]{1,0:T(8,128)S(1)}, u32[]{:S(2)}, u32[]{:S(2)}) collective-permute-start(f32[8,256]{1,0:T(8,128)S(1)} %get-tuple-element.101), channel_id=1, source_target_pairs={{0,12},{4,16},{8,20},{12,24},{16,28},{1,13},{5,17},{9,21},{13,25},... | collective-permute-start | bytes 24584 | tf_op jit(solution)/shard_map/ppermute | solution.py:385
  28.4 5.3 %collective-permute-start.8 = (f32[8,256]{1,0:T(8,128)S(1)}, f32[8,256]{1,0:T(8,128)S(1)}, u32[]{:S(2)}, u32[]{:S(2)}) collective-permute-start(f32[8,256]{1,0:T(8,128)S(1)} %get-tuple-element.101), channel_id=1, source_target_pairs={{0,8},{4,12},{8,16},{12,20},{16,24},{20,28},{1,9},{5,13},{9,17},{1... | collective-permute-start | bytes 24584 | tf_op jit(solution)/shard_map/ppermute | solution.py:385
  49.4 6.4 %collective-permute-done.6.v3 = f32[128,512]{1,0:T(8,128)} collective-permute-done((f32[128,512]{1,0:T(8,128)}, f32[128,512]{1,0:T(8,128)}, u32[]{:S(2)}, u32[]{:S(2)}) %collective-permute-start.6) | collective-permute-done | bytes 262176 | tf_op jit(solution)/shard_map/ppermute | solution.py:380
  55.9 3.9 %shard_map.114 = (f32[320,128]{1,0:T(8,128)S(1)}, f32[320,128]{1,0:T(8,128)S(1)}, bf16[512,512]{1,0:T(8,128)(2,1)S(1)}, f32[4,512,128]{2,1,0:T(8,128)S(1)}) custom-call(s32[1]{0:T(128)} %bitcast.1.p.use.bit, s32[1]{0:T(128)} %bitcast.y, bf16[4,512,128]{2,1,0:T(8,128)(2,1)S(1)} %get-tuple-element.88.uq, bf16[4,512,128]{2,1,0:T(8,128)(2,1)S(1)} %get-tuple-element.89.uk, ...), custom_call_target="tpu_custom_call" | custom-call | bytes 9800000 | tf_op jit(solution)/shard_map/pallas_call | solution.py:67
  64.6 4.2 %collective-permute-done.14.got = f32[320,128]{1,0:T(8,128)S(1)} collective-permute-done((f32[320,128]{1,0:T(8,128)S(1)}, f32[320,128]{1,0:T(8,128)S(1)}, u32[]{:S(2)}, u32[]{:S(2)}) %collective-permute-start.14) | collective-permute-done | bytes 163872 | tf_op jit(solution)/shard_map/ppermute | solution.py:392
  86.1 4.8 %collective-permute-done.20.e1 = f32[320,128]{1,0:T(8,128)S(1)} collective-permute-done((f32[320,128]{1,0:T(8,128)S(1)}, f32[320,128]{1,0:T(8,128)S(1)}, u32[]{:S(2)}, u32[]{:S(2)}) %collective-permute-start.20) | collective-permute-done | bytes 163872 | tf_op jit(solution)/shard_map/ppermute | solution.py:385
  91.9 10.4 %shard_map.118 = (f32[128,512]{1,0:T(8,128)S(1)}, f32[128,512]{1,0:T(8,128)}, f32[128,512]{1,0:T(8,128)}, f32[128,512]{1,0:T(8,128)}, f32[512,128]{1,0:T(8,128)S...) custom-call(s32[1]{0:T(128)} %bitcast.1.p.use.bit, s32[1]{0:T(128)} %bitcast.y, ...), custom_call_target="tpu_custom_call" | custom-call | bytes 33250000 | tf_op jit(solution)/shard_map/pallas_call | solution.py:67
  104.9 8.6 %collective-permute-done.29 = f32[8,256]{1,0:T(8,128)S(1)} collective-permute-done((f32[8,256]{1,0:T(8,128)S(1)}, f32[8,256]{1,0:T(8,128)S(1)}, u32[]{:S(2)}, u32[]{:S(2)}) %collective-permute-start.29) | collective-permute-done | bytes 8224 | tf_op jit(solution)/shard_map/ppermute | solution.py:385
  114.9 4.5 %collective-permute-done.27 = f32[8,256]{1,0:T(8,128)S(1)} collective-permute-done((f32[8,256]{1,0:T(8,128)S(1)}, f32[8,256]{1,0:T(8,128)S(1)}, u32[]{:S(2)}, u32[]{:S(2)}) %collective-permute-start.27) | collective-permute-done | bytes 8224 | tf_op jit(solution)/shard_map/ppermute | solution.py:385
  121.8 7.0 %collective-permute-done.30 = f32[8,256]{1,0:T(8,128)S(1)} collective-permute-done((f32[8,256]{1,0:T(8,128)S(1)}, f32[8,256]{1,0:T(8,128)S(1)}, u32[]{:S(2)}, u32[]{:S(2)}) %collective-permute-start.30) | collective-permute-done | bytes 8224 | tf_op jit(solution)/shard_map/ppermute | solution.py:385
  134.5 2.9 %collective-permute-done.26.got = f32[320,128]{1,0:T(8,128)S(1)} collective-permute-done((f32[320,128]{1,0:T(8,128)S(1)}, f32[320,128]{1,0:T(8,128)S(1)}, u32[]{:S(2)}, u32[]{:S(2)}) %collective-permute-start.26) | collective-permute-done | bytes 163872 | tf_op jit(solution)/shard_map/ppermute | solution.py:392
  137.4 3.6 %shard_map.123 = (f32[128,512]{1,0:T(8,128)S(1)}, f32[128,512]{1,0:T(8,128)S(1)}, f32[128,512]{1,0:T(8,128)S(1)}, f32[128,512]{1,0:T(8,128)S(1)}, f32[512,128]{1,0:T(8,128)S(1)}, /*index=5*/f32[8,128]{1,0:T(8,128)S(1)}) custom-call(s32[1]{0:T(128)} %bitcast.1.p.use.bit, s32[1]{0:T(128)} %bitcast.y, bf16[4,512,128]{2,1,0:T(8,128)(2,1)S(1)} %get-tuple-element.89.uk, ...), custom_call_target="tpu_custom_call" | custom-call | bytes 12250000 | tf_op jit(solution)/shard_map/pallas_call | solution.py:67
  145.0 3.2 %collective-permute-done.34.halo = f32[8,128]{1,0:T(8,128)S(1)} collective-permute-done((f32[8,128]{1,0:T(8,128)S(1)}, f32[8,128]{1,0:T(8,128)S(1)}, u32[]{:S(2)}, u32[]{:S(2)}) %collective-permute-start.34) | collective-permute-done | bytes 4128 | tf_op jit(solution)/shard_map/ppermute | solution.py:385
  151.5 3.2 %collective-permute-done.37.g3 = f32[512,128]{1,0:T(8,128)S(1)} collective-permute-done((f32[512,128]{1,0:T(8,128)S(1)}, f32[512,128]{1,0:T(8,128)S(1)}, u32[]{:S(2)}, u32[]{:S(2)}) %collective-permute-start.37) | collective-permute-done | bytes 262176 | tf_op jit(solution)/shard_map/ppermute | solution.py:380
  154.7 3.4 %collective-permute-done.36.g2 = f32[512,128]{1,0:T(8,128)S(1)} collective-permute-done((f32[512,128]{1,0:T(8,128)S(1)}, f32[512,128]{1,0:T(8,128)S(1)}, u32[]{:S(2)}, u32[]{:S(2)}) %collective-permute-start.36) | collective-permute-done | bytes 262176 | tf_op jit(solution)/shard_map/ppermute | solution.py:380
  177.1 4.7 %convolution_convert_fusion = bf16[128,4096]{1,0:T(8,128)(2,1)} fusion(bf16[128,512]{0,1:T(8,128)(2,1)S(1)} %bitcast.31, bf16[4096,512]{1,0:T(8,128)(2,1)} %param.9), kind=kOutput, calls=%fused_computation | convolution fusion | flops 537395200 | bytes 5373952 | tf_op jit(solution)/shard_map/dot_general | solution.py:57
  184.4 3.1 %collective-permute-start.45 = (f32[64,512]{1,0:T(8,128)S(1)}, f32[64,512]{1,0:T(8,128)S(1)}, u32[]{:S(2)}, u32[]{:S(2)}) collective-permute-start(f32[64,512]{1,0:T(8,128)S(1)} %get-tuple-element.159), channel_id=1, source_target_pairs={{0,4},{4,0},{8,12},{12,8},{16,20},{20,16},{24,28},{28,24},{1,5},{5... | collective-permute-start | bytes 393224 | tf_op jit(solution)/shard_map/ppermute | solution.py:392
  187.5 2.9 %collective-permute-done.45.refs_1_ = f32[64,512]{1,0:T(8,128)S(1)} collective-permute-done((f32[64,512]{1,0:T(8,128)S(1)}, f32[64,512]{1,0:T(8,128)S(1)}, u32[]{:S(2)}, u32[]{:S(2)}) %collective-permute-start.45) | collective-permute-done | bytes 131104 | tf_op jit(solution)/shard_map/ppermute | solution.py:392
  190.4 4.8 %collective-permute-start.46 = (f32[32,512]{1,0:T(8,128)S(1)}, f32[32,512]{1,0:T(8,128)S(1)}, u32[]{:S(2)}, u32[]{:S(2)}) collective-permute-start(f32[32,512]{1,0:T(8,128)S(1)} %get-tuple-element.161), channel_id=1, source_target_pairs={{0,8},{4,12},{8,0},{12,4},{16,24},{20,28},{24,16},{28,20},{1,9},{5... | collective-permute-start | bytes 196616 | tf_op jit(solution)/shard_map/ppermute | solution.py:392
  197.5 3.8 %collective-permute-start.47 = (f32[16,512]{1,0:T(8,128)S(1)}, f32[16,512]{1,0:T(8,128)S(1)}, u32[]{:S(2)}, u32[]{:S(2)}) collective-permute-start(f32[16,512]{1,0:T(8,128)S(1)} %get-tuple-element.163), channel_id=1, source_target_pairs={{0,16},{4,20},{8,24},{12,28},{16,0},{20,4},{24,8},{28,12},{1,17},{... | collective-permute-start | bytes 98312 | tf_op jit(solution)/shard_map/ppermute | solution.py:392
  201.3 4.1 %collective-permute-done.47.b = f32[16,512]{1,0:T(8,128)S(1)} collective-permute-done((f32[16,512]{1,0:T(8,128)S(1)}, f32[16,512]{1,0:T(8,128)S(1)}, u32[]{:S(2)}, u32[]{:S(2)}) %collective-permute-start.47) | collective-permute-done | bytes 32800 | tf_op jit(solution)/shard_map/ppermute | solution.py:392
  209.0 3.2 %collective-permute-start.51 = (f32[32,512]{1,0:T(8,128)S(1)}, f32[32,512]{1,0:T(8,128)S(1)}, u32[]{:S(2)}, u32[]{:S(2)}) collective-permute-start(f32[32,512]{1,0:T(8,128)S(1)} %shard_map.131.m0), channel_id=1, source_target_pairs={{0,128},{64,192},{128,0},{192,64},{1,129},{65,193},{129,1},{193,65... | collective-permute-start | bytes 196616 | tf_op jit(solution)/shard_map/ppermute | solution.py:380
  (143 shorter events, 105.3 us)
Async XLA Ops:
  17.4 30.1 %collective-permute-start.4 = (f32[128,512]{1,0:T(8,128)}, f32[128,512]{1,0:T(8,128)S(1)}, u32[]{:S(2)}, u32[]{:S(2)}) collective-permute-start(f32[128,512]{1,0:T(8,128)} %get-tuple-element.96), channel_id=1, source_target_pairs={{0,1},{1,2},{2,3},{3,0},{4,5},{5,6},{6,7},{7,4},{8,9},{9,10},{10,1... | collective-permute-start | bytes 786440 | tf_op jit(solution)/shard_map/ppermute | solution.py:380
  21.4 18.1 %collective-permute-start.9 = (f32[8,256]{1,0:T(8,128)S(1)}, f32[8,256]{1,0:T(8,128)S(1)}, u32[]{:S(2)}, u32[]{:S(2)}) collective-permute-start(f32[8,256]{1,0:T(8,128)S(1)} %get-tuple-element.101), channel_id=1, source_target_pairs={{0,12},{4,16},{8,20},{12,24},{16,28},{1,13},{5,17},{9,21},{13,25},... | collective-permute-start | bytes 24584 | tf_op jit(solution)/shard_map/ppermute | solution.py:385
  28.4 13.1 %collective-permute-start.8 = (f32[8,256]{1,0:T(8,128)S(1)}, f32[8,256]{1,0:T(8,128)S(1)}, u32[]{:S(2)}, u32[]{:S(2)}) collective-permute-start(f32[8,256]{1,0:T(8,128)S(1)} %get-tuple-element.101), channel_id=1, source_target_pairs={{0,8},{4,12},{8,16},{12,20},{16,24},{20,28},{1,9},{5,13},{9,17},{1... | collective-permute-start | bytes 24584 | tf_op jit(solution)/shard_map/ppermute | solution.py:385
  36.6 12.8 %collective-permute-start.5 = (f32[128,512]{1,0:T(8,128)}, f32[128,512]{1,0:T(8,128)}, u32[]{:S(2)}, u32[]{:S(2)}) collective-permute-start(f32[128,512]{1,0:T(8,128)} %get-tuple-element.97), channel_id=1, source_target_pairs={{0,2},{1,3},{2,0},{3,1},{4,6},{5,7},{6,4},{7,5},{8,10},{9,11},{10,... | collective-permute-start | bytes 786440 | tf_op jit(solution)/shard_map/ppermute | solution.py:380
  39.4 16.4 %collective-permute-start.6 = (f32[128,512]{1,0:T(8,128)}, f32[128,512]{1,0:T(8,128)}, u32[]{:S(2)}, u32[]{:S(2)}) collective-permute-start(f32[128,512]{1,0:T(8,128)} %get-tuple-element.98), channel_id=1, source_target_pairs={{0,3},{1,0},{2,1},{3,2},{4,7},{5,4},{6,5},{7,6},{8,11},{9,8},{10,9... | collective-permute-start | bytes 786440 | tf_op jit(solution)/shard_map/ppermute | solution.py:380
  43.5 16.5 %collective-permute-start.11 = (f32[128,512]{1,0:T(8,128)S(1)}, f32[128,512]{1,0:T(8,128)S(1)}, u32[]{:S(2)}, u32[]{:S(2)}) collective-permute-start(f32[128,512]{1,0:T(8,128)S(1)} %get-tuple-element.108), channel_id=1, source_target_pairs={{0,1},{1,2},{2,3},{3,0},{4,5},{5,6},{6,7},{7,4},{8,9},{9,10},{10,1... | collective-permute-start | bytes 786440 | tf_op jit(solution)/shard_map/ppermute | solution.py:380
  46.2 13.7 %collective-permute-start.12 = (f32[128,512]{1,0:T(8,128)S(1)}, f32[128,512]{1,0:T(8,128)S(1)}, u32[]{:S(2)}, u32[]{:S(2)}) collective-permute-start(f32[128,512]{1,0:T(8,128)S(1)} %get-tuple-element.109), channel_id=1, source_target_pairs={{0,2},{1,3},{2,0},{3,1},{4,6},{5,7},{6,4},{7,5},{8,10},{9,11},{10,... | collective-permute-start | bytes 786440 | tf_op jit(solution)/shard_map/ppermute | solution.py:380
  47.5 12.4 %collective-permute-start.13 = (f32[128,512]{1,0:T(8,128)S(1)}, f32[128,512]{1,0:T(8,128)S(1)}, u32[]{:S(2)}, u32[]{:S(2)}) collective-permute-start(f32[128,512]{1,0:T(8,128)S(1)} %get-tuple-element.110), channel_id=1, source_target_pairs={{0,3},{1,0},{2,1},{3,2},{4,7},{5,4},{6,5},{7,6},{8,11},{9,8},{10,9... | collective-permute-start | bytes 786440 | tf_op jit(solution)/shard_map/ppermute | solution.py:380
  62.5 11.5 %collective-permute-start.15 = (f32[320,128]{1,0:T(8,128)S(1)}, f32[320,128]{1,0:T(8,128)S(1)}, u32[]{:S(2)}, u32[]{:S(2)}) collective-permute-start(f32[320,128]{1,0:T(8,128)S(1)} %get-tuple-element.116), channel_id=1, source_target_pairs={{0,4},{4,0},{8,12},{12,8},{16,20},{20,16},{24,28},{28,24},{1,5},{5... | collective-permute-start | bytes 491528 | tf_op jit(solution)/shard_map/ppermute | solution.py:392
  75.6 55.5 %collective-permute-start.31 = (f32[128,1024]{1,0:T(8,128)S(1)}, f32[128,1024]{1,0:T(8,128)S(1)}, u32[]{:S(2)}, u32[]{:S(2)}) collective-permute-start(f32[128,1024]{1,0:T(8,128)S(1)} %get-tuple-element.134), channel_id=1, source_target_pairs={{0,1},{1,2},{2,3},{3,0},{4,5},{5,6},{6,7},{7,4},{8,9},{9,10},{10,1... | collective-permute-start | bytes 1572872 | tf_op jit(solution)/shard_map/ppermute | solution.py:380
  77.7 54.3 %collective-permute-start.32 = (f32[128,1024]{1,0:T(8,128)S(1)}, f32[128,1024]{1,0:T(8,128)S(1)}, u32[]{:S(2)}, u32[]{:S(2)}) collective-permute-start(f32[128,1024]{1,0:T(8,128)S(1)} %get-tuple-element.135), channel_id=1, source_target_pairs={{0,2},{1,3},{2,0},{3,1},{4,6},{5,7},{6,4},{7,5},{8,10},{9,11},{10,... | collective-permute-start | bytes 1572872 | tf_op jit(solution)/shard_map/ppermute | solution.py:380
  79.7 11.2 %collective-permute-start.20 = (f32[320,128]{1,0:T(8,128)S(1)}, f32[320,128]{1,0:T(8,128)S(1)}, u32[]{:S(2)}, u32[]{:S(2)}) collective-permute-start(f32[320,128]{1,0:T(8,128)S(1)} %add.35), channel_id=1, source_target_pairs={{16,0},{20,4},{24,8},{28,12},{17,1},{21,5},{25,9},{29,13},{18,2},{... | collective-permute-start | bytes 491528 | tf_op jit(solution)/shard_map/ppermute | solution.py:385
  81.0 10.9 %collective-permute-start.19 = (f32[320,128]{1,0:T(8,128)S(1)}, f32[320,128]{1,0:T(8,128)S(1)}, u32[]{:S(2)}, u32[]{:S(2)}) collective-permute-start(f32[320,128]{1,0:T(8,128)S(1)} %add.35), channel_id=1, source_target_pairs={{8,0},{12,4},{16,8},{20,12},{24,16},{28,20},{9,1},{13,5},{17,9},{2... | collective-permute-start | bytes 491528 | tf_op jit(solution)/shard_map/ppermute | solution.py:385
  90.9 43.2 %collective-permute-start.33 = (f32[128,1024]{1,0:T(8,128)S(1)}, f32[128,1024]{1,0:T(8,128)S(1)}, u32[]{:S(2)}, u32[]{:S(2)}) collective-permute-start(f32[128,1024]{1,0:T(8,128)S(1)} %get-tuple-element.136), channel_id=1, source_target_pairs={{0,3},{1,0},{2,1},{3,2},{4,7},{5,4},{6,5},{7,6},{8,11},{9,8},{10,9... | collective-permute-start | bytes 1572872 | tf_op jit(solution)/shard_map/ppermute | solution.py:380
  102.3 11.2 %collective-permute-start.29 = (f32[8,256]{1,0:T(8,128)S(1)}, f32[8,256]{1,0:T(8,128)S(1)}, u32[]{:S(2)}, u32[]{:S(2)}) collective-permute-start(f32[8,256]{1,0:T(8,128)S(1)} %get-tuple-element.131), channel_id=1, source_target_pairs={{12,0},{16,4},{20,8},{24,12},{28,16},{13,1},{17,5},{21,9},{25,13},... | collective-permute-start | bytes 24584 | tf_op jit(solution)/shard_map/ppermute | solution.py:385
  103.6 11.2 %collective-permute-start.28 = (f32[8,256]{1,0:T(8,128)S(1)}, f32[8,256]{1,0:T(8,128)S(1)}, u32[]{:S(2)}, u32[]{:S(2)}) collective-permute-start(f32[8,256]{1,0:T(8,128)S(1)} %get-tuple-element.131), channel_id=1, source_target_pairs={{8,0},{12,4},{16,8},{20,12},{24,16},{28,20},{9,1},{13,5},{17,9},{2... | collective-permute-start | bytes 24584 | tf_op jit(solution)/shard_map/ppermute | solution.py:385
  120.6 23.5 %collective-permute-start.23 = (f32[128,512]{1,0:T(8,128)}, f32[128,512]{1,0:T(8,128)S(1)}, u32[]{:S(2)}, u32[]{:S(2)}) collective-permute-start(f32[128,512]{1,0:T(8,128)} %get-tuple-element.123), channel_id=1, source_target_pairs={{0,1},{1,2},{2,3},{3,0},{4,5},{5,6},{6,7},{7,4},{8,9},{9,10},{10,1... | collective-permute-start | bytes 786440 | tf_op jit(solution)/shard_map/ppermute | solution.py:380
  128.8 15.3 %collective-permute-start.24 = (f32[128,512]{1,0:T(8,128)}, f32[128,512]{1,0:T(8,128)S(1)}, u32[]{:S(2)}, u32[]{:S(2)}) collective-permute-start(f32[128,512]{1,0:T(8,128)} %get-tuple-element.124), channel_id=1, source_target_pairs={{0,2},{1,3},{2,0},{3,1},{4,6},{5,7},{6,4},{7,5},{8,10},{9,11},{10,... | collective-permute-start | bytes 786440 | tf_op jit(solution)/shard_map/ppermute | solution.py:380
  131.1 13.0 %collective-permute-start.25 = (f32[128,512]{1,0:T(8,128)}, f32[128,512]{1,0:T(8,128)S(1)}, u32[]{:S(2)}, u32[]{:S(2)}) collective-permute-start(f32[128,512]{1,0:T(8,128)} %get-tuple-element.125), channel_id=1, source_target_pairs={{0,3},{1,0},{2,1},{3,2},{4,7},{5,4},{6,5},{7,6},{8,11},{9,8},{10,9... | collective-permute-start | bytes 786440 | tf_op jit(solution)/shard_map/ppermute | solution.py:380
  166.2 15.5 %collective-permute-start.40 = (f32[128,512]{1,0:T(8,128)}, f32[128,512]{1,0:T(8,128)S(1)}, u32[]{:S(2)}, u32[]{:S(2)}) collective-permute-start(f32[128,512]{1,0:T(8,128)} %copy-done.8), channel_id=1, source_target_pairs={{0,2},{1,3},{2,0},{3,1},{4,6},{5,7},{6,4},{7,5},{8,10},{9,11},{10,... | collective-permute-start | bytes 786440 | tf_op jit(solution)/shard_map/ppermute | solution.py:380
  168.4 13.4 %collective-permute-start.41 = (f32[128,512]{1,0:T(8,128)}, f32[128,512]{1,0:T(8,128)S(1)}, u32[]{:S(2)}, u32[]{:S(2)}) collective-permute-start(f32[128,512]{1,0:T(8,128)} %copy-done.7), channel_id=1, source_target_pairs={{0,3},{1,0},{2,1},{3,2},{4,7},{5,4},{6,5},{7,6},{8,11},{9,8},{10,9... | collective-permute-start | bytes 786440 | tf_op jit(solution)/shard_map/ppermute | solution.py:380
  168.8 13.7 %collective-permute-start.42 = (f32[128,512]{1,0:T(8,128)}, f32[128,512]{1,0:T(8,128)S(1)}, u32[]{:S(2)}, u32[]{:S(2)}) collective-permute-start(f32[128,512]{1,0:T(8,128)} %copy-done.11), channel_id=1, source_target_pairs={{0,64},{64,128},{128,192},{192,0},{1,65},{65,129},{129,193},{193,1... | collective-permute-start | bytes 786440 | tf_op jit(solution)/shard_map/ppermute | solution.py:380
  170.6 13.8 %collective-permute-start.43 = (f32[128,512]{1,0:T(8,128)}, f32[128,512]{1,0:T(8,128)S(1)}, u32[]{:S(2)}, u32[]{:S(2)}) collective-permute-start(f32[128,512]{1,0:T(8,128)} %copy-done.10), channel_id=1, source_target_pairs={{0,128},{64,192},{128,0},{192,64},{1,129},{65,193},{129,1},{193,65... | collective-permute-start | bytes 786440 | tf_op jit(solution)/shard_map/ppermute | solution.py:380
  174.4 10.0 %collective-permute-start.44 = (f32[128,512]{1,0:T(8,128)S(1)}, f32[128,512]{1,0:T(8,128)S(1)}, u32[]{:S(2)}, u32[]{:S(2)}) collective-permute-start(f32[128,512]{1,0:T(8,128)S(1)} %get-tuple-element.157), channel_id=1, source_target_pairs={{0,192},{64,0},{128,64},{192,128},{1,193},{65,1},{129,65},{193,129... | collective-permute-start | bytes 786440 | tf_op jit(solution)/shard_map/ppermute | solution.py:380
  (41 other events, 436.7 us)
where the time goes:
time: 222 us; the launch traced here: 219 us
  starting transfers between devices  97.7 us (44%)
  waiting for transfers between devices  79.7 us (36%)
  Pallas kernels  30 us (14%)
  matrix products  7.97 us (4%)
    ppermute x27, starting transfers between devices, shift(): return lax.ppermute(value, axis, [(i, (i + by) % n) for i in range(n)])  44.2 us
    ppermute x15, starting transfers between devices, shift_open(): lax.ppermute(value, axis, [(i, i + by) for i in range(n) if 0 <= i + by <...  31.2 us
    ppermute x15, waiting for transfers between devices, shift_open(): lax.ppermute(value, axis, [(i, i + by) for i in range(n) if 0 <= i + by <...  31.1 us
    pallas_call x22, Pallas kernels, run(): pl.pallas_call(kernel, out_shape=[jax.ShapeDtypeStruct(s, d) for s, d in...  30 us
    ppermute x27, waiting for transfers between devices, shift(): return lax.ppermute(value, axis, [(i, (i + by) % n) for i in range(n)])  24.7 us
    ppermute x10, waiting for transfers between devices, swap(): return lax.ppermute(value, axis, [(i, i ^ mask) for i in range(n)])  21.8 us
    ppermute x10, starting transfers between devices, swap(): return lax.ppermute(value, axis, [(i, i ^ mask) for i in range(n)])  18.7 us
    dot_general x1, matrix products, mm_nt(): lax.dot_general(a, b, (((1,), (1,)), ((), ())), preferred_element_type=f32)  4.66 us
  transfers between devices with their start and end apart: 53, of which 26 were waited for; matrix products, arithmetic and copies ran while one was open for 2% of the time, Pallas kernels for 12%

commit v1 on v0

--- a/solution.py
+++ b/solution.py
@@ -236,8 +236,7 @@
 
 
 def local_kernel(
-    p, y, uq, uk, vb, dn, inv, etot, own, got, sel_q, w,
-    o0, o1, o2, o3, dq, gv, dk, gtot, dk_acc, states, out,
+    p, uq, uk, vb, dn, inv, etot, own, got, sel_q, w, out, dq, gv, dk, gtot, dk_acc, states
 ):
     lane = lax.broadcasted_iota(jnp.int32, (TS, 128), 1)
     gtot[...] = jnp.zeros_like(gtot)
@@ -284,12 +283,10 @@
         return 0
 
     lax.fori_loop(0, HG, one, 0)
-    for s, o in enumerate((o0, o1, o2, o3)):
-        o[...] = out[turned(y, s)]
 
 
 def key_kernel(
-    p, y, uk, vb, gv_in, dq, dk, own, got, egtot, sel_k,
+    p, y, uk, vb, gv_in, dq, dk, own, got, egtot, out, sel_k,
     o0, o1, o2, o3, gm, edge, states, gv,
 ):
     lane = lax.broadcasted_iota(jnp.int32, (TS, 128), 1)
@@ -309,7 +306,8 @@
     lax.fori_loop(0, HG, one, 0)
     edge[...] = gm[:8]
     for s, o in enumerate((o0, o1, o2, o3)):
-        o[...] = gv[group_lanes(turned(y, s), T)]
+        o[:, : HG * V] = out[turned(y, s)]
+        o[:, HG * V :] = gv[group_lanes(turned(y, s), T)]
 
 
 def conv_back_kernel(y, gm, halo, cw, gp, pad):
@@ -370,9 +368,11 @@
                 rows[at, 256 + half * 128 : 256 + half * 128 + 128] = k
 
 
-def rows_kernel(y, b0, b1, b2, b3, rows):
+def rows_kernel(y, b0, b1, b2, b3, out, grad):
     for s, b in enumerate((b0, b1, b2, b3)):
-        rows[:, group_lanes(turned(y, -s), HG * V)] = b[...].astype(bf16)
+        cols = group_lanes(turned(y, -s), HG * V)
+        out[:, cols] = b[:, : HG * V].astype(bf16)
+        grad[:, cols] = b[:, HG * V :].astype(bf16)
 
 
 def shift(value, axis, by):
@@ -393,9 +393,9 @@
 
 
 def totals_scan(tot, sign):
-    near = sum(shift_open(tot, "z", sign * s) for s in (1, 2, 3))
-    far = shift_open(near + tot, "z", sign * 4)
-    return near + far
+    before = shift_open(tot, "z", sign)
+    before = before + shift_open(before + tot, "z", 2 * sign)
+    return before + shift_open(before + tot, "z", 4 * sign)
 
 
 def across_pairs(keep, got, sign):
@@ -424,19 +424,18 @@
     local_x = tokens[0]
     wide = HG * V
 
+    by_head = [((T, wide), f32)] * NY
+    v_all = swap_y(run(pack_kernel, by_head, y1, values[0], smem=1))
     projected = jnp.dot(local_x, qk_weight, preferred_element_type=f32)
     halo = lax.ppermute(
         projected[T - 8 :], ("z", "y"), [(i, i + 1) for i in range(NZ * NY - 1)]
     )
-    by_head = [((T, wide), f32)] * NY
-    v_packed = run(pack_kernel, by_head, y1, after(values[0], projected), smem=1)
     c_packed = run(pack_kernel, by_head, y1, after(cotangent[0], projected), smem=1)
     mixed = run(
-        mix_kernel, [((T, 128), f32)] * NY, y1, projected, halo, conv_weight, smem=1,
+        mix_kernel, [((T, 128), f32)] * NY, y1, after(projected, *v_all), halo, conv_weight, smem=1,
         scratch=[pltpu.VMEM((T + 8, 512), f32), pltpu.VMEM((NY, T, 128), f32)],
     )
     mixed = swap_y(mixed)
-    v_all = swap_y(lax.optimization_barrier((*v_packed, *mixed))[:NY])
     uq, uk, tot = timed(
         2.6, prepare_kernel,
         [((HG, TS, 128), bf16), ((HG, TS, 128), bf16), ((8, EP), f32)],
@@ -459,40 +458,32 @@
     earlier = across_pairs(keep, pair, 1)
     g_later = across_pairs(g_keep, g_pair, -1)
     own, got = back_to_pair(keep, after(pair, g_pair), earlier, parity)
-    own = after(own, *g_later)
     g_own, g_got = back_to_pair(g_keep, g_pair, g_later, 1 - parity)
-
-    x_packed = timed(
-        1.5, pack_columns_kernel, [((T, NZ * T), f32)] * NY, y1, after(local_x, g_keep), smem=1
-    )
-    (flipped,) = timed(
-        1.9, flip_kernel, [((NZ * T, TS), bf16)], y1, *swap_y(x_packed), smem=1
-    )
 
     states = pltpu.VMEM((HG, EP, V), bf16)
     square = ((TS, 128), f32)
-    *out, dq, gv_in, dk, gtot = timed(
+    out, dq, gv_in, dk, gtot = timed(
         9.5, local_kernel,
-        by_head + [square, ((TS, wide), f32), square, ((8, EP), f32)],
-        parity, y1, uq, uk, vb, dn, inv, etot, own, got, sel_q, w, smem=2,
-        scratch=[pltpu.VMEM((TS, 128), f32), states, pltpu.VMEM((NY, T, wide), f32)],
-    )
+        [((NY, T, wide), f32), square, ((TS, wide), f32), square, ((8, EP), f32)],
+        parity, uq, uk, vb, dn, inv, etot, own, got, sel_q, w, smem=1,
+        scratch=[pltpu.VMEM((TS, 128), f32), states],
+    )
+    x_packed = timed(
+        1.5, pack_columns_kernel, [((T, NZ * T), f32)] * NY, y1, after(local_x, etot), smem=1
+    )
+    x_all = swap_y(lax.optimization_barrier((*x_packed, gtot))[:NY])
+    (flipped,) = timed(1.9, flip_kernel, [((NZ * T, TS), bf16)], y1, *x_all, smem=1)
     egtot = totals_scan(gtot, -1)
 
-    def token_rows(blocks):
-        return run(rows_kernel, [((T, H * V), bf16)], y1, *swap_y(blocks), smem=1)[0]
-
-    mixed_out = token_rows(out)
-    egtot = after(egtot, flipped)
-    *gv, gm, edge = timed(
-        3.5, key_kernel, by_head + [square, ((8, 128), f32)],
-        parity, y1, uk, vb, gv_in, dq, dk, g_own, g_got, egtot, sel_k, smem=2,
+    *both, gm, edge = timed(
+        3.5, key_kernel, [((T, 2 * wide), f32)] * NY + [square, ((8, 128), f32)],
+        parity, y1, uk, vb, gv_in, dq, dk, g_own, g_got, egtot, out, sel_k, smem=2,
         scratch=[states, pltpu.VMEM((TS, wide), f32)],
     )
     taps = conv_weight.shape[0]
     cw = jnp.transpose(conv_weight.reshape(taps, 2, NY, 64), (0, 2, 1, 3)).reshape(taps, 512)
     (gp,) = run(
-        conv_back_kernel, [square], y1, after(gm, mixed_out), shift_open(edge, "z", -1), cw, smem=1,
+        conv_back_kernel, [square], y1, gm, shift_open(edge, "z", -1), cw, smem=1,
         scratch=[pltpu.VMEM((TS + 8, 128), f32)],
     )
     blocks = [gp] + [shift(gp, "y", s) for s in (1, 2, 3)]
@@ -510,9 +501,12 @@
         after(grad_own, parts[0]).reshape(T, NY, 2, 64), (0, 2, 1, 3)
     ).reshape(T, 512)
     grad_x = mm_nt(own_rows, qk_weight).astype(bf16)
-    grad_values = token_rows(lax.optimization_barrier((*gv, parts[0]))[:NY])
+    both = swap_y(lax.optimization_barrier((*both, keep))[:NY])
+    mixed_out, grad_values = run(
+        rows_kernel, [((T, H * V), bf16)] * 2, y1, *both, smem=1
+    )
     parts = [parts[0]] + [shift(parts[s], "x", s) for s in (1, 2, 3)]
-    parts[0] = after(parts[0], grad_x, grad_values)
+    parts[0] = after(parts[0], grad_x)
     for mask in (1, 2, 4):
         n = 64 // mask
         bit = lax.rem(lax.div(z, mask), 2).reshape(1)
@@ -520,6 +514,7 @@
             split_z_kernel, [((n, 512), f32), ((n, 512), f32)], bit, *parts, smem=1
         )
         parts = [keep, swap(send, "z", mask)]
+    parts[0] = after(parts[0], grad_values)
     (pair_rows,) = run(
         stack_kernel, [((32, 512), f32)], core.reshape(1), *parts,
         *[swap(a, "core", 1) for a in parts], smem=1,

time: 222 us -> 213 us (0.959); the launches traced: 219 us -> 212 us
  waiting for transfers between devices: 79.7 us -> 66.5 us
  local copies, waits for them, and re-layouts: 1.93 us -> 13.3 us
  starting transfers between devices: 97.7 us -> 92.6 us
    unnamed x24 -> x50, local copies, waits for them, and re-layouts: 1.61 us -> 13 us
    ppermute x10, waiting for transfers between devices: 21.8 us -> 15.2 us  [swap(): return lax.ppermute(value, axis, [(i, i ^ mask) for i in range(n)])]
    ppermute x27 -> x24, starting transfers between devices: 44.2 us -> 39.1 us  [shift(): return lax.ppermute(value, axis, [(i, (i + by) % n) for i in range(n)])]
    ppermute x27 -> x24, waiting for transfers between devices: 24.7 us -> 21.3 us  [shift(): return lax.ppermute(value, axis, [(i, (i + by) % n) for i in range(n)])]
    ppermute x15 -> x13, starting transfers between devices: 31.2 us -> 32.4 us  [shift_open(): lax.ppermute(value, axis, [(i, i + by) for i in range(n) if 0 <= i + by <...]
    ppermute x15 -> x13, waiting for transfers between devices: 31.1 us -> 30 us  [shift_open(): lax.ppermute(value, axis, [(i, i + by) for i in range(n) if 0 <= i + by <...]
    pallas_call x22 -> x21, Pallas kernels: 30 us -> 30.4 us  [run(): pl.pallas_call(kernel, out_shape=[jax.ShapeDtypeStruct(s, d) for s, d in...]
  transfers between devices with their start and end apart: 53 -> 48, of which waited for: 26 -> 24; matrix products, arithmetic and copies ran while one was open for 2% -> 4% of each run, Pallas kernels for 12% -> 7%
where the time goes in v1:
time: 213 us; the launch traced here: 212 us
  starting transfers between devices  92.6 us (43%)
  waiting for transfers between devices  66.5 us (31%)
  Pallas kernels  30.4 us (14%)
  local copies, waits for them, and re-layouts  13.3 us (6%)
  matrix products  7.88 us (4%)
    ppermute x24, starting transfers between devices, shift(): return lax.ppermute(value, axis, [(i, (i + by) % n) for i in range(n)])  39.1 us
    ppermute x13, starting transfers between devices, shift_open(): lax.ppermute(value, axis, [(i, i + by) for i in range(n) if 0 <= i + by <...  32.4 us
    pallas_call x21, Pallas kernels, run(): pl.pallas_call(kernel, out_shape=[jax.ShapeDtypeStruct(s, d) for s, d in...  30.4 us
    ppermute x13, waiting for transfers between devices, shift_open(): lax.ppermute(value, axis, [(i, i + by) for i in range(n) if 0 <= i + by <...  30 us
    ppermute x24, waiting for transfers between devices, shift(): return lax.ppermute(value, axis, [(i, (i + by) % n) for i in range(n)])  21.3 us
    ppermute x10, starting transfers between devices, swap(): return lax.ppermute(value, axis, [(i, i ^ mask) for i in range(n)])  17.7 us
    ppermute x10, waiting for transfers between devices, swap(): return lax.ppermute(value, axis, [(i, i ^ mask) for i in range(n)])  15.2 us
    unnamed x50, local copies, waits for them, and re-layouts  13 us
  transfers between devices with their start and end apart: 48, of which 24 were waited for; matrix products, arithmetic and copies ran while one was open for 4% of the time, Pallas kernels for 7%

profile of v1, /device:TPU:8, one launch (start us, length us, event | category | flops | bytes accessed | tf_op | source)
XLA Modules:
  0.0 211.9 jit_solution(11845873762765274663)
XLA Ops:
  7.4 3.2 %fusion.projected = f32[128,512]{1,0:T(8,128)S(1)} fusion(bf16[4096,512]{1,0:T(8,128)(2,1)} %param.9, bf16[1,128,4096]{2,1,0:T(8,128)(2,1)} %param.8), kind=kOutput, calls=%fused_computation.3 | convolution fusion | flops 536870912 | bytes 5505024 | tf_op jit(solution)/shard_map/dot_general | solution.py:429
  10.7 3.4 %collective-permute-start.3 = (f32[8,512]{1,0:T(8,128)S(1)}, f32[8,512]{1,0:T(8,128)S(1)}, u32[]{:S(2)}, u32[]{:S(2)}) collective-permute-start(f32[8,512]{1,0:T(8,128)S(1)} %slice.4), channel_id=1, source_target_pairs={{0,1},{1,2},{2,3},{3,4},{4,5},{5,6},{6,7},{7,8},{8,9},{9,10},{10,1... | collective-permute-start | bytes 49160 | tf_op jit(solution)/shard_map/ppermute | solution.py:430
  14.8 3.4 %collective-permute-done.2.v3 = f32[128,512]{1,0:T(8,128)S(1)} collective-permute-done((f32[128,512]{1,0:T(8,128)S(1)}, f32[128,512]{1,0:T(8,128)S(1)}, u32[]{:S(2)}, u32[]{:S(2)}) %collective-permute-start.2) | collective-permute-done | bytes 262176 | tf_op jit(solution)/shard_map/ppermute | solution.py:380
  29.0 4.0 %collective-permute-start.7 = (f32[8,256]{1,0:T(8,128)S(1)}, f32[8,256]{1,0:T(8,128)S(1)}, u32[]{:S(2)}, u32[]{:S(2)}) collective-permute-start(f32[8,256]{1,0:T(8,128)S(1)} %get-tuple-element.94), channel_id=1, source_target_pairs={{0,4},{4,8},{8,12},{12,16},{16,20},{20,24},{24,28},{1,5},{5,9},{9,... | collective-permute-start | bytes 24584 | tf_op jit(solution)/shard_map/ppermute | solution.py:385
  34.4 5.5 %collective-permute-start.8 = (f32[8,256]{1,0:T(8,128)S(1)}, f32[8,256]{1,0:T(8,128)S(1)}, u32[]{:S(2)}, u32[]{:S(2)}) collective-permute-start(f32[8,256]{1,0:T(8,128)S(1)} %add.30), channel_id=1, source_target_pairs={{0,8},{4,12},{8,16},{12,20},{16,24},{20,28},{1,9},{5,13},{9,17},{1... | collective-permute-start | bytes 24584 | tf_op jit(solution)/shard_map/ppermute | solution.py:385
  45.8 8.1 %collective-permute-start.9 = (f32[8,256]{1,0:T(8,128)S(1)}, f32[8,256]{1,0:T(8,128)S(1)}, u32[]{:S(2)}, u32[]{:S(2)}) collective-permute-start(f32[8,256]{1,0:T(8,128)S(1)} %get-tuple-element.160), channel_id=1, source_target_pairs={{0,16},{4,20},{8,24},{12,28},{1,17},{5,21},{9,25},{13,29},{2,18},{... | collective-permute-start | bytes 24584 | tf_op jit(solution)/shard_map/ppermute | solution.py:385
  57.7 2.9 %shard_map.114 = (f32[320,128]{1,0:T(8,128)S(1)}, f32[320,128]{1,0:T(8,128)S(1)}, bf16[512,512]{1,0:T(8,128)(2,1)S(1)}, f32[4,512,128]{2,1,0:T(8,128)S(1)}) custom-call(s32[1]{0:T(128)} %bitcast.1.p.use.bit, s32[1]{0:T(128)} %bitcast.y, bf16[4,512,128]{2,1,0:T(8,128)(2,1)S(1)} %get-tuple-element.91.uq, bf16[4,512,128]{2,1,0:T(8,128)(2,1)S(1)} %get-tuple-element.90.uk, ...), custom_call_target="tpu_custom_call" | custom-call | bytes 9800000 | tf_op jit(solution)/shard_map/pallas_call | solution.py:67
  70.3 2.9 %collective-permute-start.16 = (f32[320,128]{1,0:T(8,128)S(1)}, f32[320,128]{1,0:T(8,128)S(1)}, u32[]{:S(2)}, u32[]{:S(2)}) collective-permute-start(f32[320,128]{1,0:T(8,128)S(1)} %add.34), channel_id=1, source_target_pairs={{0,16},{4,20},{8,24},{12,28},{1,17},{5,21},{9,25},{13,29},{2,18},{... | collective-permute-start | bytes 491528 | tf_op jit(solution)/shard_map/ppermute | solution.py:385
  74.6 2.8 %collective-permute-done.16.e1 = f32[320,128]{1,0:T(8,128)S(1)} collective-permute-done((f32[320,128]{1,0:T(8,128)S(1)}, f32[320,128]{1,0:T(8,128)S(1)}, u32[]{:S(2)}, u32[]{:S(2)}) %collective-permute-start.16) | collective-permute-done | bytes 163872 | tf_op jit(solution)/shard_map/ppermute | solution.py:385
  84.8 9.5 %shard_map.118 = (f32[4,128,512]{2,1,0:T(8,128)S(1)}, f32[512,128]{1,0:T(8,128)S(1)}, f32[512,512]{1,0:T(8,128)S(1)}, f32[512,128]{1,0:T(8,128)S(1)}, f32[8,256]{1,0:T(8,128)S(1)}) custom-call(s32[1]{0:T(128)} %bitcast.1.p.use.bit, bf16[4,512,128]{2,1,0:T(8,128)(2,1)S(1)} %get-tuple-element.91.uq, bf16[4,512,128]{2,1,0:T(8,128)(2,1)S(1)} %get-tuple-element.90.uk, ...), custom_call_target="tpu_custom_call" | custom-call | bytes 33250000 | tf_op jit(solution)/shard_map/pallas_call | solution.py:67
  100.6 6.7 %collective-permute-done.19.e0 = f32[320,128]{1,0:T(8,128)S(1)} collective-permute-done((f32[320,128]{1,0:T(8,128)S(1)}, f32[320,128]{1,0:T(8,128)S(1)}, u32[]{:S(2)}, u32[]{:S(2)}) %collective-permute-start.19) | collective-permute-done | bytes 163872 | tf_op jit(solution)/shard_map/ppermute | solution.py:385
  112.4 3.5 %collective-permute-start.22 = (f32[320,128]{1,0:T(8,128)S(1)}, f32[320,128]{1,0:T(8,128)S(1)}, u32[]{:S(2)}, u32[]{:S(2)}) collective-permute-start(f32[320,128]{1,0:T(8,128)S(1)} %get-tuple-element.118), channel_id=1, source_target_pairs={{0,4},{4,0},{8,12},{12,8},{16,20},{20,16},{24,28},{28,24},{1,5},{5... | collective-permute-start | bytes 491528 | tf_op jit(solution)/shard_map/ppermute | solution.py:392
  115.9 4.8 %collective-permute-done.24 = f32[8,256]{1,0:T(8,128)S(1)} collective-permute-done((f32[8,256]{1,0:T(8,128)S(1)}, f32[8,256]{1,0:T(8,128)S(1)}, u32[]{:S(2)}, u32[]{:S(2)}) %collective-permute-start.24) | collective-permute-done | bytes 8224 | tf_op jit(solution)/shard_map/ppermute | solution.py:385
  121.9 8.2 %collective-permute-done.25 = f32[8,256]{1,0:T(8,128)S(1)} collective-permute-done((f32[8,256]{1,0:T(8,128)S(1)}, f32[8,256]{1,0:T(8,128)S(1)}, u32[]{:S(2)}, u32[]{:S(2)}) %collective-permute-start.25) | collective-permute-done | bytes 8224 | tf_op jit(solution)/shard_map/ppermute | solution.py:385
  130.1 3.7 %shard_map.120 = (f32[128,1024]{1,0:T(8,128)S(1)}, f32[128,1024]{1,0:T(8,128)S(1)}, f32[128,1024]{1,0:T(8,128)S(1)}, f32[128,1024]{1,0:T(8,128)S(1)}, f32[512,128]{1,0:T(8,128)S(1)}, /*index=5*/f32[8,128]{1,0:T(8,128)S(1)}) custom-call(s32[1]{0:T(128)} %bitcast.1.p.use.bit, s32[1]{0:T(128)} %bitcast.y, bf16[4,512,128]{2,1,0:T(8,128)(2,1)S(1)} %get-tuple-element.90.uk, ...), custom_call_target="tpu_custom_call" | custom-call | bytes 12250000 | tf_op jit(solution)/shard_map/pallas_call | solution.py:67
  137.7 4.0 %collective-permute-done.26.halo = f32[8,128]{1,0:T(8,128)S(1)} collective-permute-done((f32[8,128]{1,0:T(8,128)S(1)}, f32[8,128]{1,0:T(8,128)S(1)}, u32[]{:S(2)}, u32[]{:S(2)}) %collective-permute-start.26) | collective-permute-done | bytes 4128 | tf_op jit(solution)/shard_map/ppermute | solution.py:385
  156.6 2.9 %collective-permute-done.36.b = f32[512,512]{1,0:T(8,128)S(1)} collective-permute-done((f32[512,512]{1,0:T(8,128)}, f32[512,512]{1,0:T(8,128)S(1)}, u32[]{:S(2)}, u32[]{:S(2)}) %collective-permute-start.36) | collective-permute-done | bytes 1048608 | tf_op jit(solution)/shard_map/ppermute | solution.py:392
  173.1 4.7 %convolution_convert_fusion = bf16[128,4096]{1,0:T(8,128)(2,1)} fusion(bf16[128,512]{0,1:T(8,128)(2,1)S(1)} %bitcast.29, bf16[4096,512]{1,0:T(8,128)(2,1)} %param.9), kind=kOutput, calls=%fused_computation | convolution fusion | flops 537395200 | bytes 5373952 | tf_op jit(solution)/shard_map/dot_general | solution.py:57
  183.3 2.9 %collective-permute-done.40.refs_1_ = f32[64,512]{1,0:T(8,128)S(1)} collective-permute-done((f32[64,512]{1,0:T(8,128)S(1)}, f32[64,512]{1,0:T(8,128)S(1)}, u32[]{:S(2)}, u32[]{:S(2)}) %collective-permute-start.40) | collective-permute-done | bytes 131104 | tf_op jit(solution)/shard_map/ppermute | solution.py:392
  186.2 3.6 %collective-permute-start.41 = (f32[32,512]{1,0:T(8,128)S(1)}, f32[32,512]{1,0:T(8,128)S(1)}, u32[]{:S(2)}, u32[]{:S(2)}) collective-permute-start(f32[32,512]{1,0:T(8,128)S(1)} %get-tuple-element.154), channel_id=1, source_target_pairs={{0,8},{4,12},{8,0},{12,4},{16,24},{20,28},{24,16},{28,20},{1,9},{5... | collective-permute-start | bytes 196616 | tf_op jit(solution)/shard_map/ppermute | solution.py:392
  192.1 3.2 %collective-permute-start.42 = (f32[16,512]{1,0:T(8,128)S(1)}, f32[16,512]{1,0:T(8,128)S(1)}, u32[]{:S(2)}, u32[]{:S(2)}) collective-permute-start(f32[16,512]{1,0:T(8,128)S(1)} %get-tuple-element.157), channel_id=1, source_target_pairs={{0,16},{4,20},{8,24},{12,28},{16,0},{20,4},{24,8},{28,12},{1,17},{... | collective-permute-start | bytes 98312 | tf_op jit(solution)/shard_map/ppermute | solution.py:392
  196.3 4.0 %collective-permute-done.42.b = f32[16,512]{1,0:T(8,128)S(1)} collective-permute-done((f32[16,512]{1,0:T(8,128)S(1)}, f32[16,512]{1,0:T(8,128)S(1)}, u32[]{:S(2)}, u32[]{:S(2)}) %collective-permute-start.42) | collective-permute-done | bytes 32800 | tf_op jit(solution)/shard_map/ppermute | solution.py:392
  201.5 3.8 %collective-permute-start.45 = (f32[32,512]{1,0:T(8,128)S(1)}, f32[32,512]{1,0:T(8,128)S(1)}, u32[]{:S(2)}, u32[]{:S(2)}) collective-permute-start(f32[32,512]{1,0:T(8,128)S(1)} %shard_map.130.m0), channel_id=1, source_target_pairs={{0,64},{64,128},{128,192},{192,0},{1,65},{65,129},{129,193},{193,1... | collective-permute-start | bytes 196616 | tf_op jit(solution)/shard_map/ppermute | solution.py:380
  208.1 3.0 %collective-permute-done.46.m2 = f32[32,512]{1,0:T(8,128)S(1)} collective-permute-done((f32[32,512]{1,0:T(8,128)S(1)}, f32[32,512]{1,0:T(8,128)S(1)}, u32[]{:S(2)}, u32[]{:S(2)}) %collective-permute-start.46) | collective-permute-done | bytes 65568 | tf_op jit(solution)/shard_map/ppermute | solution.py:380
  (160 shorter events, 106.4 us)
Async XLA Ops:
  2.5 11.6 %collective-permute-start = (f32[128,512]{1,0:T(8,128)S(1)}, f32[128,512]{1,0:T(8,128)S(1)}, u32[]{:S(2)}, u32[]{:S(2)}) collective-permute-start(f32[128,512]{1,0:T(8,128)S(1)} %get-tuple-element.82), channel_id=1, source_target_pairs={{0,1},{1,2},{2,3},{3,0},{4,5},{5,6},{6,7},{7,4},{8,9},{9,10},{10,1... | collective-permute-start | bytes 786440 | tf_op jit(solution)/shard_map/ppermute | solution.py:380
  4.1 10.7 %collective-permute-start.1 = (f32[128,512]{1,0:T(8,128)S(1)}, f32[128,512]{1,0:T(8,128)S(1)}, u32[]{:S(2)}, u32[]{:S(2)}) collective-permute-start(f32[128,512]{1,0:T(8,128)S(1)} %get-tuple-element.83), channel_id=1, source_target_pairs={{0,2},{1,3},{2,0},{3,1},{4,6},{5,7},{6,4},{7,5},{8,10},{9,11},{10,... | collective-permute-start | bytes 786440 | tf_op jit(solution)/shard_map/ppermute | solution.py:380
  6.8 11.4 %collective-permute-start.2 = (f32[128,512]{1,0:T(8,128)S(1)}, f32[128,512]{1,0:T(8,128)S(1)}, u32[]{:S(2)}, u32[]{:S(2)}) collective-permute-start(f32[128,512]{1,0:T(8,128)S(1)} %get-tuple-element.84), channel_id=1, source_target_pairs={{0,3},{1,0},{2,1},{3,2},{4,7},{5,4},{6,5},{7,6},{8,11},{9,8},{10,9... | collective-permute-start | bytes 786440 | tf_op jit(solution)/shard_map/ppermute | solution.py:380
  34.4 11.5 %collective-permute-start.8 = (f32[8,256]{1,0:T(8,128)S(1)}, f32[8,256]{1,0:T(8,128)S(1)}, u32[]{:S(2)}, u32[]{:S(2)}) collective-permute-start(f32[8,256]{1,0:T(8,128)S(1)} %add.30), channel_id=1, source_target_pairs={{0,8},{4,12},{8,16},{12,20},{16,24},{20,28},{1,9},{5,13},{9,17},{1... | collective-permute-start | bytes 24584 | tf_op jit(solution)/shard_map/ppermute | solution.py:385
  40.8 20.2 %collective-permute-start.10 = (f32[128,512]{1,0:T(8,128)}, f32[128,512]{1,0:T(8,128)S(1)}, u32[]{:S(2)}, u32[]{:S(2)}) collective-permute-start(f32[128,512]{1,0:T(8,128)} %get-tuple-element.101), channel_id=1, source_target_pairs={{0,1},{1,2},{2,3},{3,0},{4,5},{5,6},{6,7},{7,4},{8,9},{9,10},{10,1... | collective-permute-start | bytes 786440 | tf_op jit(solution)/shard_map/ppermute | solution.py:380
  41.2 19.8 %collective-permute-start.11 = (f32[128,512]{1,0:T(8,128)}, f32[128,512]{1,0:T(8,128)S(1)}, u32[]{:S(2)}, u32[]{:S(2)}) collective-permute-start(f32[128,512]{1,0:T(8,128)} %get-tuple-element.102), channel_id=1, source_target_pairs={{0,2},{1,3},{2,0},{3,1},{4,6},{5,7},{6,4},{7,5},{8,10},{9,11},{10,... | collective-permute-start | bytes 786440 | tf_op jit(solution)/shard_map/ppermute | solution.py:380
  43.6 18.1 %collective-permute-start.12 = (f32[128,512]{1,0:T(8,128)}, f32[128,512]{1,0:T(8,128)S(1)}, u32[]{:S(2)}, u32[]{:S(2)}) collective-permute-start(f32[128,512]{1,0:T(8,128)} %get-tuple-element.103), channel_id=1, source_target_pairs={{0,3},{1,0},{2,1},{3,2},{4,7},{5,4},{6,5},{7,6},{8,11},{9,8},{10,9... | collective-permute-start | bytes 786440 | tf_op jit(solution)/shard_map/ppermute | solution.py:380
  45.8 14.8 %collective-permute-start.9 = (f32[8,256]{1,0:T(8,128)S(1)}, f32[8,256]{1,0:T(8,128)S(1)}, u32[]{:S(2)}, u32[]{:S(2)}) collective-permute-start(f32[8,256]{1,0:T(8,128)S(1)} %get-tuple-element.160), channel_id=1, source_target_pairs={{0,16},{4,20},{8,24},{12,28},{1,17},{5,21},{9,25},{13,29},{2,18},{... | collective-permute-start | bytes 24584 | tf_op jit(solution)/shard_map/ppermute | solution.py:385
  94.3 51.0 %collective-permute-start.30 = (f32[128,1024]{1,0:T(8,128)}, f32[128,1024]{1,0:T(8,128)S(1)}, u32[]{:S(2)}, u32[]{:S(2)}) collective-permute-start(f32[128,1024]{1,0:T(8,128)} %get-tuple-element.133), channel_id=1, source_target_pairs={{0,1},{1,2},{2,3},{3,0},{4,5},{5,6},{6,7},{7,4},{8,9},{9,10},{10,1... | collective-permute-start | bytes 1572872 | tf_op jit(solution)/shard_map/ppermute | solution.py:380
  95.4 11.9 %collective-permute-start.19 = (f32[320,128]{1,0:T(8,128)S(1)}, f32[320,128]{1,0:T(8,128)S(1)}, u32[]{:S(2)}, u32[]{:S(2)}) collective-permute-start(f32[320,128]{1,0:T(8,128)S(1)} %add.35), channel_id=1, source_target_pairs={{8,0},{12,4},{16,8},{20,12},{24,16},{28,20},{9,1},{13,5},{17,9},{2... | collective-permute-start | bytes 491528 | tf_op jit(solution)/shard_map/ppermute | solution.py:385
  96.7 13.6 %collective-permute-start.20 = (f32[320,128]{1,0:T(8,128)S(1)}, f32[320,128]{1,0:T(8,128)S(1)}, u32[]{:S(2)}, u32[]{:S(2)}) collective-permute-start(f32[320,128]{1,0:T(8,128)S(1)} %add.35), channel_id=1, source_target_pairs={{16,0},{20,4},{24,8},{28,12},{17,1},{21,5},{25,9},{29,13},{18,2},{... | collective-permute-start | bytes 491528 | tf_op jit(solution)/shard_map/ppermute | solution.py:385
  98.0 14.3 %collective-permute-start.21 = (f32[320,128]{1,0:T(8,128)S(1)}, f32[320,128]{1,0:T(8,128)S(1)}, u32[]{:S(2)}, u32[]{:S(2)}) collective-permute-start(f32[320,128]{1,0:T(8,128)S(1)} %add.35), channel_id=1, source_target_pairs={{24,0},{28,4},{25,1},{29,5},{26,2},{30,6},{27,3},{31,7},{56,32},{6... | collective-permute-start | bytes 491528 | tf_op jit(solution)/shard_map/ppermute | solution.py:385
  107.3 38.7 %collective-permute-start.31 = (f32[128,1024]{1,0:T(8,128)}, f32[128,1024]{1,0:T(8,128)}, u32[]{:S(2)}, u32[]{:S(2)}) collective-permute-start(f32[128,1024]{1,0:T(8,128)} %get-tuple-element.134), channel_id=1, source_target_pairs={{0,2},{1,3},{2,0},{3,1},{4,6},{5,7},{6,4},{7,5},{8,10},{9,11},{10,... | collective-permute-start | bytes 1572872 | tf_op jit(solution)/shard_map/ppermute | solution.py:380
  108.4 37.7 %collective-permute-start.32 = (f32[128,1024]{1,0:T(8,128)}, f32[128,1024]{1,0:T(8,128)}, u32[]{:S(2)}, u32[]{:S(2)}) collective-permute-start(f32[128,1024]{1,0:T(8,128)} %get-tuple-element.135), channel_id=1, source_target_pairs={{0,3},{1,0},{2,1},{3,2},{4,7},{5,4},{6,5},{7,6},{8,11},{9,8},{10,9... | collective-permute-start | bytes 1572872 | tf_op jit(solution)/shard_map/ppermute | solution.py:380
  110.4 10.3 %collective-permute-start.24 = (f32[8,256]{1,0:T(8,128)S(1)}, f32[8,256]{1,0:T(8,128)S(1)}, u32[]{:S(2)}, u32[]{:S(2)}) collective-permute-start(f32[8,256]{1,0:T(8,128)S(1)} %add.36), channel_id=1, source_target_pairs={{8,0},{12,4},{16,8},{20,12},{24,16},{28,20},{9,1},{13,5},{17,9},{2... | collective-permute-start | bytes 24584 | tf_op jit(solution)/shard_map/ppermute | solution.py:385
  112.4 17.7 %collective-permute-start.22 = (f32[320,128]{1,0:T(8,128)S(1)}, f32[320,128]{1,0:T(8,128)S(1)}, u32[]{:S(2)}, u32[]{:S(2)}) collective-permute-start(f32[320,128]{1,0:T(8,128)S(1)} %get-tuple-element.118), channel_id=1, source_target_pairs={{0,4},{4,0},{8,12},{12,8},{16,20},{20,16},{24,28},{28,24},{1,5},{5... | collective-permute-start | bytes 491528 | tf_op jit(solution)/shard_map/ppermute | solution.py:392
  120.6 9.4 %collective-permute-start.25 = (f32[8,256]{1,0:T(8,128)S(1)}, f32[8,256]{1,0:T(8,128)S(1)}, u32[]{:S(2)}, u32[]{:S(2)}) collective-permute-start(f32[8,256]{1,0:T(8,128)S(1)} %get-tuple-element.158), channel_id=1, source_target_pairs={{16,0},{20,4},{24,8},{28,12},{17,1},{21,5},{25,9},{29,13},{18,2},{... | collective-permute-start | bytes 24584 | tf_op jit(solution)/shard_map/ppermute | solution.py:385
  145.3 9.2 %collective-permute-start.29 = (f32[512,128]{1,0:T(8,128)S(1)}, f32[512,128]{1,0:T(8,128)S(1)}, u32[]{:S(2)}, u32[]{:S(2)}) collective-permute-start(f32[512,128]{1,0:T(8,128)S(1)} %shard_map.121.g0), channel_id=1, source_target_pairs={{0,3},{1,0},{2,1},{3,2},{4,7},{5,4},{6,5},{7,6},{8,11},{9,8},{10,9... | collective-permute-start | bytes 786440 | tf_op jit(solution)/shard_map/ppermute | solution.py:380
  161.0 9.8 %collective-permute-start.37 = (f32[128,512]{1,0:T(8,128)}, f32[128,512]{1,0:T(8,128)S(1)}, u32[]{:S(2)}, u32[]{:S(2)}) collective-permute-start(f32[128,512]{1,0:T(8,128)} %get-tuple-element.148), channel_id=1, source_target_pairs={{0,64},{64,128},{128,192},{192,0},{1,65},{65,129},{129,193},{193,1... | collective-permute-start | bytes 786440 | tf_op jit(solution)/shard_map/ppermute | solution.py:380
  162.5 32.8 %collective-permute-start.33 = (f32[128,1024]{1,0:T(8,128)}, f32[128,1024]{1,0:T(8,128)S(1)}, u32[]{:S(2)}, u32[]{:S(2)}) collective-permute-start(f32[128,1024]{1,0:T(8,128)} %copy-done.23), channel_id=1, source_target_pairs={{0,1},{1,2},{2,3},{3,0},{4,5},{5,6},{6,7},{7,4},{8,9},{9,10},{10,1... | collective-permute-start | bytes 1572872 | tf_op jit(solution)/shard_map/ppermute | solution.py:380
  163.1 32.1 %collective-permute-start.34 = (f32[128,1024]{1,0:T(8,128)}, f32[128,1024]{1,0:T(8,128)S(1)}, u32[]{:S(2)}, u32[]{:S(2)}) collective-permute-start(f32[128,1024]{1,0:T(8,128)} %copy-done.22), channel_id=1, source_target_pairs={{0,2},{1,3},{2,0},{3,1},{4,6},{5,7},{6,4},{7,5},{8,10},{9,11},{10,... | collective-permute-start | bytes 1572872 | tf_op jit(solution)/shard_map/ppermute | solution.py:380
  164.5 30.7 %collective-permute-start.35 = (f32[128,1024]{1,0:T(8,128)}, f32[128,1024]{1,0:T(8,128)S(1)}, u32[]{:S(2)}, u32[]{:S(2)}) collective-permute-start(f32[128,1024]{1,0:T(8,128)} %copy-done.21), channel_id=1, source_target_pairs={{0,3},{1,0},{2,1},{3,2},{4,7},{5,4},{6,5},{7,6},{8,11},{9,8},{10,9... | collective-permute-start | bytes 1572872 | tf_op jit(solution)/shard_map/ppermute | solution.py:380
  166.8 11.0 %collective-permute-start.38 = (f32[128,512]{1,0:T(8,128)}, f32[128,512]{1,0:T(8,128)S(1)}, u32[]{:S(2)}, u32[]{:S(2)}) collective-permute-start(f32[128,512]{1,0:T(8,128)} %copy-done.24), channel_id=1, source_target_pairs={{0,128},{64,192},{128,0},{192,64},{1,129},{65,193},{129,1},{193,65... | collective-permute-start | bytes 786440 | tf_op jit(solution)/shard_map/ppermute | solution.py:380
  170.8 9.7 %collective-permute-start.39 = (f32[128,512]{1,0:T(8,128)S(1)}, f32[128,512]{1,0:T(8,128)S(1)}, u32[]{:S(2)}, u32[]{:S(2)}) collective-permute-start(f32[128,512]{1,0:T(8,128)S(1)} %get-tuple-element.150), channel_id=1, source_target_pairs={{0,192},{64,0},{128,64},{192,128},{1,193},{65,1},{129,65},{193,129... | collective-permute-start | bytes 786440 | tf_op jit(solution)/shard_map/ppermute | solution.py:380
  (49 other events, 471.4 us)

commit v2 on v1

--- a/solution.py
+++ b/solution.py
@@ -61,14 +61,19 @@
     return lax.dot_general(a, b, (((0,), (0,)), ((), ())), preferred_element_type=f32)
 
 
-def run(kernel, outs, *args, scratch=(), smem=0, us=0.5):
+def run(kernel, outs, *args, scratch=(), smem=0, us=0.5, placed=(), far_outs=()):
     vm = pl.BlockSpec(memory_space=pltpu.VMEM)
     sm = pl.BlockSpec(memory_space=pltpu.SMEM)
     return pl.pallas_call(
         kernel,
         out_shape=[jax.ShapeDtypeStruct(s, d) for s, d in outs],
-        in_specs=[sm] * smem + [vm] * (len(args) - smem),
-        out_specs=[vm] * len(outs),
+        in_specs=[
+            sm if i < smem else pl.BlockSpec(memory_space=pltpu.HBM) if i in placed else vm
+            for i in range(len(args))
+        ],
+        out_specs=[
+            pl.BlockSpec(memory_space=pltpu.HBM) if i in far_outs else vm for i in range(len(outs))
+        ],
         scratch_shapes=list(scratch),
         compiler_params=pltpu.CompilerParams(vmem_limit_bytes=12 << 20),
         cost_estimate=pl.CostEstimate(
@@ -116,6 +121,13 @@
 def pack_kernel(y, a, *outs):
     for s, o in enumerate(outs):
         o[...] = a[:, group_lanes(turned(y, s), HG * V)].astype(f32)
+
+
+def fetch(blocks, buffer, sems):
+    copies = [pltpu.make_async_copy(b, buffer.at[s], sems.at[s]) for s, b in enumerate(blocks)]
+    for c in copies:
+        c.start()
+    return copies
 
 
 def after(value, *others):
@@ -185,9 +197,13 @@
     send[...] = scratch[1 - p]
 
 
-def state_kernel(p, y, uq, uk, v0, v1, v2, v3, sel_k, w, keep, send, vb, rs, scratch):
-    for s, v in enumerate((v0, v1, v2, v3)):
-        vb[group_lanes(turned(y, -s), T)] = v[...].astype(bf16)
+def state_kernel(
+    p, y, uq, uk, v0, v1, v2, v3, sel_k, w, keep, send, vb, rs, scratch, buffer, sems
+):
+    copies = fetch((v0, v1, v2, v3), buffer, sems)
+    for s in range(NY):
+        copies[s].wait()
+        vb[group_lanes(turned(y, -s), T)] = buffer[s].astype(bf16)
 
     def one(h, _):
         rk = (features(uk[h], sel_k[...]) * w[0:1]).astype(bf16)
@@ -204,15 +220,19 @@
     halves(scratch, p[0], keep, send)
 
 
-def denom_kernel(p, y, uq, rs, etot, c0, c1, c2, c3, sel_q, w, keep, send, dn, inv, scratch):
+def denom_kernel(
+    p, y, uq, rs, etot, c0, c1, c2, c3, sel_q, w, keep, send, dn, inv, scratch, buffer, sems
+):
+    for c in fetch((c0, c1, c2, c3), buffer, sems):
+        c.wait()
     def one(h, _):
         rq = features(uq[h], sel_q[...])
         den = rs[h] + jnp.sum(rq * etot[pl.ds(h, 1)], 1, keepdims=True)
         iv = 1.0 / den
         inv[h] = iv
-        for s, c in enumerate((c0, c1, c2, c3)):
+        for s in range(NY):
             rows = group_lanes(turned(y, -s), T)
-            dn[rows, lanes(h)] = (c[:, lanes(h)] * inv[h, rows]).astype(bf16)
+            dn[rows, lanes(h)] = (buffer[s, :, lanes(h)] * inv[h, rows]).astype(bf16)
         s = mm_tn((rq * w[0:1]).astype(bf16), dn[:, lanes(h)])
         scratch[lax.div(h, 2), pl.ds(pl.multiple_of(lax.rem(h, 2) * E, E), E)] = s[:E]
         return 0
@@ -287,9 +307,15 @@
 
 def key_kernel(
     p, y, uk, vb, gv_in, dq, dk, own, got, egtot, out, sel_k,
-    o0, o1, o2, o3, gm, edge, states, gv,
+    o0, o1, o2, o3, gm, edge, states, gv, sems,
 ):
     lane = lax.broadcasted_iota(jnp.int32, (TS, 128), 1)
+    copies = [
+        pltpu.make_async_copy(out.at[turned(y, s)], o.at[:, pl.ds(0, HG * V)], sems.at[s])
+        for s, o in enumerate((o0, o1, o2, o3))
+    ]
+    for c in copies:
+        c.start()
     fill_states(p[0], own, got, states)
     gm[...] = dq[...] + dk[...]
 
@@ -306,8 +332,14 @@
     lax.fori_loop(0, HG, one, 0)
     edge[...] = gm[:8]
     for s, o in enumerate((o0, o1, o2, o3)):
-        o[:, : HG * V] = out[turned(y, s)]
-        o[:, HG * V :] = gv[group_lanes(turned(y, s), T)]
+        copies.append(
+            pltpu.make_async_copy(
+                gv.at[group_lanes(turned(y, s), T)], o.at[:, pl.ds(HG * V, HG * V)], sems.at[NY + s]
+            )
+        )
+        copies[-1].start()
+    for c in copies:
+        c.wait()
 
 
 def conv_back_kernel(y, gm, halo, cw, gp, pad):
@@ -430,9 +462,8 @@
     halo = lax.ppermute(
         projected[T - 8 :], ("z", "y"), [(i, i + 1) for i in range(NZ * NY - 1)]
     )
-    c_packed = run(pack_kernel, by_head, y1, after(cotangent[0], projected), smem=1)
     mixed = run(
-        mix_kernel, [((T, 128), f32)] * NY, y1, after(projected, *v_all), halo, conv_weight, smem=1,
+        mix_kernel, [((T, 128), f32)] * NY, y1, after(projected, *v_all[1:]), halo, conv_weight, smem=1,
         scratch=[pltpu.VMEM((T + 8, 512), f32), pltpu.VMEM((NY, T, 128), f32)],
     )
     mixed = swap_y(mixed)
@@ -441,17 +472,22 @@
         [((HG, TS, 128), bf16), ((HG, TS, 128), bf16), ((8, EP), f32)],
         y1, *mixed, sel_k, w, smem=1, scratch=[pltpu.VMEM((TS, 128), f32)],
     )
-    c_all = swap_y(lax.optimization_barrier((*c_packed, tot))[:NY])
+    c_all = swap_y(run(pack_kernel, by_head, y1, after(cotangent[0], tot), smem=1))
     etot = totals_scan(tot, 1)
     half = ((2 * E, V), f32)
-    half_scratch = [pltpu.VMEM((2, 2 * E, V), f32)]
+    half_scratch = [
+        pltpu.VMEM((2, 2 * E, V), f32), pltpu.VMEM((NY, T, wide), f32),
+        pltpu.SemaphoreType.DMA((NY,)),
+    ]
     keep, send, vb, rs = timed(
         2.8, state_kernel, [half, half, ((TS, wide), bf16), ((HG, TS, V), f32)],
         parity, y1, uq, uk, *v_all, sel_k, w, smem=2, scratch=half_scratch,
+        placed=(4, 5, 6, 7),
     )
     g_keep, g_send, dn, inv = timed(
         2.4, denom_kernel, [half, half, ((TS, wide), bf16), ((HG, TS, V), f32)],
         parity, y1, uq, rs, etot, *c_all, sel_q, w, smem=2, scratch=half_scratch,
+        placed=(5, 6, 7, 8),
     )
     pair = swap(after(send, etot), "z", 1)
     g_pair = swap(g_send, "z", 1)
@@ -459,6 +495,7 @@
     g_later = across_pairs(g_keep, g_pair, -1)
     own, got = back_to_pair(keep, after(pair, g_pair), earlier, parity)
     g_own, g_got = back_to_pair(g_keep, g_pair, g_later, 1 - parity)
+    own = after(own, g_own)
 
     states = pltpu.VMEM((HG, EP, V), bf16)
     square = ((TS, 128), f32)
@@ -471,14 +508,15 @@
     x_packed = timed(
         1.5, pack_columns_kernel, [((T, NZ * T), f32)] * NY, y1, after(local_x, etot), smem=1
     )
-    x_all = swap_y(lax.optimization_barrier((*x_packed, gtot))[:NY])
+    x_all = swap_y(lax.optimization_barrier((*x_packed, g_keep))[:NY])
     (flipped,) = timed(1.9, flip_kernel, [((NZ * T, TS), bf16)], y1, *x_all, smem=1)
     egtot = totals_scan(gtot, -1)
 
     *both, gm, edge = timed(
         3.5, key_kernel, [((T, 2 * wide), f32)] * NY + [square, ((8, 128), f32)],
         parity, y1, uk, vb, gv_in, dq, dk, g_own, g_got, egtot, out, sel_k, smem=2,
-        scratch=[states, pltpu.VMEM((TS, wide), f32)],
+        scratch=[states, pltpu.VMEM((TS, wide), f32), pltpu.SemaphoreType.DMA((2 * NY,))],
+        far_outs=(0, 1, 2, 3),
     )
     taps = conv_weight.shape[0]
     cw = jnp.transpose(conv_weight.reshape(taps, 2, NY, 64), (0, 2, 1, 3)).reshape(taps, 512)
@@ -501,12 +539,12 @@
         after(grad_own, parts[0]).reshape(T, NY, 2, 64), (0, 2, 1, 3)
     ).reshape(T, 512)
     grad_x = mm_nt(own_rows, qk_weight).astype(bf16)
-    both = swap_y(lax.optimization_barrier((*both, keep))[:NY])
+    parts = [parts[0]] + [shift(parts[s], "x", s) for s in (1, 2, 3)]
+    parts[0] = after(parts[0], grad_x)
+    both = swap_y(lax.optimization_barrier((*both, parts[1]))[:NY])
     mixed_out, grad_values = run(
         rows_kernel, [((T, H * V), bf16)] * 2, y1, *both, smem=1
     )
-    parts = [parts[0]] + [shift(parts[s], "x", s) for s in (1, 2, 3)]
-    parts[0] = after(parts[0], grad_x)
     for mask in (1, 2, 4):
         n = 64 // mask
         bit = lax.rem(lax.div(z, mask), 2).reshape(1)
@@ -514,12 +552,12 @@
             split_z_kernel, [((n, 512), f32), ((n, 512), f32)], bit, *parts, smem=1
         )
         parts = [keep, swap(send, "z", mask)]
-    parts[0] = after(parts[0], grad_values)
     (pair_rows,) = run(
         stack_kernel, [((32, 512), f32)], core.reshape(1), *parts,
         *[swap(a, "core", 1) for a in parts], smem=1,
     )
     stacks = [pair_rows] + [shift(pair_rows, "x", s) for s in (1, 2, 3)]
+    stacks[0] = after(stacks[0], grad_values)
     (weight_grad,) = run(finish_kernel, [((T, 512), f32)], x.reshape(1), *stacks, smem=1)
 
     return (mixed_out[None], grad_x[None], grad_values[None], weight_grad)

time: 213 us -> 204 us (0.958)
  waiting for transfers between devices: 66.5 us -> 58.4 us
  local copies, waits for them, and re-layouts: 13.3 us -> 11 us
    ppermute x13, waiting for transfers between devices: 30 us -> 25.2 us  [shift_open(): lax.ppermute(value, axis, [(i, i + by) for i in range(n) if 0 <= i + by <...]
    ppermute x24, waiting for transfers between devices: 21.3 us -> 18.4 us  [shift(): return lax.ppermute(value, axis, [(i, (i + by) % n) for i in range(n)])]
    unnamed x50 -> x44, local copies, waits for them, and re-layouts: 13 us -> 10.7 us
  transfers between devices with their start and end apart: 48 -> 48, of which waited for: 24 -> 21; matrix products, arithmetic and copies ran while one was open for 4% -> 4% of each run, Pallas kernels for 7% -> 12%
where the time goes in v2:
time: 204 us
  starting transfers between devices  94.2 us (46%)
  waiting for transfers between devices  58.4 us (29%)
  Pallas kernels  31 us (15%)
  local copies, waits for them, and re-layouts  11 us (5%)
  matrix products  7.88 us (4%)
    ppermute x24, starting transfers between devices, shift(): return lax.ppermute(value, axis, [(i, (i + by) % n) for i in range(n)])  41 us
    ppermute x13, starting transfers between devices, shift_open(): lax.ppermute(value, axis, [(i, i + by) for i in range(n) if 0 <= i + by <...  32.5 us
    pallas_call x21, Pallas kernels, run(): pl.pallas_call(kernel, out_shape=[jax.ShapeDtypeStruct(s, d) for s, d in...  31 us
    ppermute x13, waiting for transfers between devices, shift_open(): lax.ppermute(value, axis, [(i, i + by) for i in range(n) if 0 <= i + by <...  25.2 us
    ppermute x24, waiting for transfers between devices, shift(): return lax.ppermute(value, axis, [(i, (i + by) % n) for i in range(n)])  18.4 us
    ppermute x10, starting transfers between devices, swap(): return lax.ppermute(value, axis, [(i, i ^ mask) for i in range(n)])  17.3 us
    ppermute x10, waiting for transfers between devices, swap(): return lax.ppermute(value, axis, [(i, i ^ mask) for i in range(n)])  14.8 us
    unnamed x44, local copies, waits for them, and re-layouts  10.7 us
  transfers between devices with their start and end apart: 48, of which 21 were waited for; matrix products, arithmetic and copies ran while one was open for 4% of the time, Pallas kernels for 12%

profile of v2, /device:TPU:8, one launch (start us, length us, event | category | flops | bytes accessed | tf_op | source)
XLA Modules:
  0.0 203.7 jit_solution(664415323969795270)
XLA Ops:
  7.4 3.2 %fusion.projected = f32[128,512]{1,0:T(8,128)S(1)} fusion(bf16[4096,512]{1,0:T(8,128)(2,1)} %param.9, bf16[1,128,4096]{2,1,0:T(8,128)(2,1)} %param.8), kind=kOutput, calls=%fused_computation.3 | convolution fusion | flops 536870912 | bytes 5505024 | tf_op jit(solution)/shard_map/dot_general | solution.py:461
  10.7 3.4 %collective-permute-start.3 = (f32[8,512]{1,0:T(8,128)S(1)}, f32[8,512]{1,0:T(8,128)S(1)}, u32[]{:S(2)}, u32[]{:S(2)}) collective-permute-start(f32[8,512]{1,0:T(8,128)S(1)} %slice.4), channel_id=1, source_target_pairs={{0,1},{1,2},{2,3},{3,4},{4,5},{5,6},{6,7},{7,8},{8,9},{9,10},{10,1... | collective-permute-start | bytes 49160 | tf_op jit(solution)/shard_map/ppermute | solution.py:462
  14.8 3.4 %collective-permute-done.2.v3 = f32[128,512]{1,0:T(8,128)S(1)} collective-permute-done((f32[128,512]{1,0:T(8,128)S(1)}, f32[128,512]{1,0:T(8,128)S(1)}, u32[]{:S(2)}, u32[]{:S(2)}) %collective-permute-start.2) | collective-permute-done | bytes 262176 | tf_op jit(solution)/shard_map/ppermute | solution.py:412
  29.0 4.0 %collective-permute-start.7 = (f32[8,256]{1,0:T(8,128)S(1)}, f32[8,256]{1,0:T(8,128)S(1)}, u32[]{:S(2)}, u32[]{:S(2)}) collective-permute-start(f32[8,256]{1,0:T(8,128)S(1)} %get-tuple-element.91), channel_id=1, source_target_pairs={{0,4},{4,8},{8,12},{12,16},{16,20},{20,24},{24,28},{1,5},{5,9},{9,... | collective-permute-start | bytes 24584 | tf_op jit(solution)/shard_map/ppermute | solution.py:417
  34.4 5.5 %collective-permute-start.8 = (f32[8,256]{1,0:T(8,128)S(1)}, f32[8,256]{1,0:T(8,128)S(1)}, u32[]{:S(2)}, u32[]{:S(2)}) collective-permute-start(f32[8,256]{1,0:T(8,128)S(1)} %add.30), channel_id=1, source_target_pairs={{0,8},{4,12},{8,16},{12,20},{16,24},{20,28},{1,9},{5,13},{9,17},{1... | collective-permute-start | bytes 24584 | tf_op jit(solution)/shard_map/ppermute | solution.py:417
  45.8 8.0 %collective-permute-start.9 = (f32[8,256]{1,0:T(8,128)S(1)}, f32[8,256]{1,0:T(8,128)S(1)}, u32[]{:S(2)}, u32[]{:S(2)}) collective-permute-start(f32[8,256]{1,0:T(8,128)S(1)} %get-tuple-element.154), channel_id=1, source_target_pairs={{0,16},{4,20},{8,24},{12,28},{1,17},{5,21},{9,25},{13,29},{2,18},{... | collective-permute-start | bytes 24584 | tf_op jit(solution)/shard_map/ppermute | solution.py:417
  57.7 3.0 %shard_map.114 = (f32[320,128]{1,0:T(8,128)S(1)}, f32[320,128]{1,0:T(8,128)S(1)}, bf16[512,512]{1,0:T(8,128)(2,1)S(1)}, f32[4,512,128]{2,1,0:T(8,128)S(1)}) custom-call(s32[1]{0:T(128)} %bitcast.1.p.use.bit, s32[1]{0:T(128)} %bitcast.y, bf16[4,512,128]{2,1,0:T(8,128)(2,1)S(1)} %get-tuple-element.87.uq, bf16[4,512,128]{2,1,0:T(8,128)(2,1)S(1)} %get-tuple-element.86.uk, ...), custom_call_target="tpu_custom_call" | custom-call | bytes 9800000 | tf_op jit(solution)/shard_map/pallas_call | solution.py:67
  70.6 2.8 %collective-permute-start.16 = (f32[320,128]{1,0:T(8,128)S(1)}, f32[320,128]{1,0:T(8,128)S(1)}, u32[]{:S(2)}, u32[]{:S(2)}) collective-permute-start(f32[320,128]{1,0:T(8,128)S(1)} %add.34), channel_id=1, source_target_pairs={{0,16},{4,20},{8,24},{12,28},{1,17},{5,21},{9,25},{13,29},{2,18},{... | collective-permute-start | bytes 491528 | tf_op jit(solution)/shard_map/ppermute | solution.py:417
  80.4 4.6 %collective-permute-start.21 = (f32[320,128]{1,0:T(8,128)S(1)}, f32[320,128]{1,0:T(8,128)S(1)}, u32[]{:S(2)}, u32[]{:S(2)}) collective-permute-start(f32[320,128]{1,0:T(8,128)S(1)} %get-tuple-element.108), channel_id=1, source_target_pairs={{0,4},{4,0},{8,12},{12,8},{16,20},{20,16},{24,28},{28,24},{1,5},{5... | collective-permute-start | bytes 491528 | tf_op jit(solution)/shard_map/ppermute | solution.py:424
  92.4 9.5 %shard_map.119 = (f32[4,128,512]{2,1,0:T(8,128)S(1)}, f32[512,128]{1,0:T(8,128)S(1)}, f32[512,512]{1,0:T(8,128)S(1)}, f32[512,128]{1,0:T(8,128)S(1)}, f32[8,256]{1,0:T(8,128)S(1)}) custom-call(s32[1]{0:T(128)} %bitcast.1.p.use.bit, bf16[4,512,128]{2,1,0:T(8,128)(2,1)S(1)} %get-tuple-element.87.uq, bf16[4,512,128]{2,1,0:T(8,128)(2,1)S(1)} %get-tuple-element.86.uk, ...), custom_call_target="tpu_custom_call" | custom-call | bytes 33250000 | tf_op jit(solution)/shard_map/pallas_call | solution.py:67
  103.2 5.3 %collective-permute-done.23 = f32[8,256]{1,0:T(8,128)S(1)} collective-permute-done((f32[8,256]{1,0:T(8,128)S(1)}, f32[8,256]{1,0:T(8,128)S(1)}, u32[]{:S(2)}, u32[]{:S(2)}) %collective-permute-start.23) | collective-permute-done | bytes 8224 | tf_op jit(solution)/shard_map/ppermute | solution.py:417
  111.9 3.2 %collective-permute-done.24 = f32[8,256]{1,0:T(8,128)S(1)} collective-permute-done((f32[8,256]{1,0:T(8,128)S(1)}, f32[8,256]{1,0:T(8,128)S(1)}, u32[]{:S(2)}, u32[]{:S(2)}) %collective-permute-start.24) | collective-permute-done | bytes 8224 | tf_op jit(solution)/shard_map/ppermute | solution.py:417
  116.4 8.2 %collective-permute-done.25 = f32[8,256]{1,0:T(8,128)S(1)} collective-permute-done((f32[8,256]{1,0:T(8,128)S(1)}, f32[8,256]{1,0:T(8,128)S(1)}, u32[]{:S(2)}, u32[]{:S(2)}) %collective-permute-start.25) | collective-permute-done | bytes 8224 | tf_op jit(solution)/shard_map/ppermute | solution.py:417
  124.5 3.9 %shard_map.120 = (f32[128,1024]{1,0:T(8,128)S(1)}, f32[128,1024]{1,0:T(8,128)S(1)}, f32[128,1024]{1,0:T(8,128)S(1)}, f32[128,1024]{1,0:T(8,128)S(1)}, f32[512,128]{1,0:T(8,128)S(1)}, /*index=5*/f32[8,128]{1,0:T(8,128)S(1)}) custom-call(s32[1]{0:T(128)} %bitcast.1.p.use.bit, s32[1]{0:T(128)} %bitcast.y, bf16[4,512,128]{2,1,0:T(8,128)(2,1)S(1)} %get-tuple-element.86.uk, ...), custom_call_target="tpu_custom_call" | custom-call | bytes 12250000 | tf_op jit(solution)/shard_map/pallas_call | solution.py:67
  131.6 4.0 %collective-permute-done.26.halo = f32[8,128]{1,0:T(8,128)S(1)} collective-permute-done((f32[8,128]{1,0:T(8,128)S(1)}, f32[8,128]{1,0:T(8,128)S(1)}, u32[]{:S(2)}, u32[]{:S(2)}) %collective-permute-start.26) | collective-permute-done | bytes 4128 | tf_op jit(solution)/shard_map/ppermute | solution.py:417
  143.3 2.8 %collective-permute-done.28.g2 = f32[512,128]{1,0:T(8,128)S(1)} collective-permute-done((f32[512,128]{1,0:T(8,128)S(1)}, f32[512,128]{1,0:T(8,128)S(1)}, u32[]{:S(2)}, u32[]{:S(2)}) %collective-permute-start.28) | collective-permute-done | bytes 262176 | tf_op jit(solution)/shard_map/ppermute | solution.py:412
  150.9 2.9 %collective-permute-done.33.b = f32[512,512]{1,0:T(8,128)S(1)} collective-permute-done((f32[512,512]{1,0:T(8,128)}, f32[512,512]{1,0:T(8,128)S(1)}, u32[]{:S(2)}, u32[]{:S(2)}) %collective-permute-start.33) | collective-permute-done | bytes 1048608 | tf_op jit(solution)/shard_map/ppermute | solution.py:424
  156.2 2.8 %collective-permute-start.38 = (f32[128,512]{1,0:T(8,128)}, f32[128,512]{1,0:T(8,128)S(1)}, u32[]{:S(2)}, u32[]{:S(2)}) collective-permute-start(f32[128,512]{1,0:T(8,128)} %get-tuple-element.143), channel_id=1, source_target_pairs={{0,128},{64,192},{128,0},{192,64},{1,129},{65,193},{129,1},{193,65... | collective-permute-start | bytes 786440 | tf_op jit(solution)/shard_map/ppermute | solution.py:412
  160.5 3.7 %collective-permute-done.34.refs_1_ = f32[128,512]{1,0:T(8,128)S(1)} collective-permute-done((f32[128,512]{1,0:T(8,128)S(1)}, f32[128,512]{1,0:T(8,128)S(1)}, u32[]{:S(2)}, u32[]{:S(2)}) %collective-permute-start.34) | collective-permute-done | bytes 262176 | tf_op jit(solution)/shard_map/ppermute | solution.py:412
  168.4 4.6 %convolution_convert_fusion = bf16[128,4096]{1,0:T(8,128)(2,1)} fusion(bf16[128,512]{0,1:T(8,128)(2,1)S(1)} %bitcast.29, bf16[4096,512]{1,0:T(8,128)(2,1)} %param.9), kind=kOutput, calls=%fused_computation | convolution fusion | flops 537395200 | bytes 5373952 | tf_op jit(solution)/shard_map/dot_general | solution.py:57
  175.1 3.1 %collective-permute-done.40.refs_1_ = f32[64,512]{1,0:T(8,128)S(1)} collective-permute-done((f32[64,512]{1,0:T(8,128)S(1)}, f32[64,512]{1,0:T(8,128)S(1)}, u32[]{:S(2)}, u32[]{:S(2)}) %collective-permute-start.40) | collective-permute-done | bytes 131104 | tf_op jit(solution)/shard_map/ppermute | solution.py:424
  178.2 3.5 %collective-permute-start.41 = (f32[32,512]{1,0:T(8,128)S(1)}, f32[32,512]{1,0:T(8,128)S(1)}, u32[]{:S(2)}, u32[]{:S(2)}) collective-permute-start(f32[32,512]{1,0:T(8,128)S(1)} %get-tuple-element.148), channel_id=1, source_target_pairs={{0,8},{4,12},{8,0},{12,4},{16,24},{20,28},{24,16},{28,20},{1,9},{5... | collective-permute-start | bytes 196616 | tf_op jit(solution)/shard_map/ppermute | solution.py:424
  183.9 2.9 %collective-permute-start.42 = (f32[16,512]{1,0:T(8,128)S(1)}, f32[16,512]{1,0:T(8,128)S(1)}, u32[]{:S(2)}, u32[]{:S(2)}) collective-permute-start(f32[16,512]{1,0:T(8,128)S(1)} %get-tuple-element.150), channel_id=1, source_target_pairs={{0,16},{4,20},{8,24},{12,28},{16,0},{20,4},{24,8},{28,12},{1,17},{... | collective-permute-start | bytes 98312 | tf_op jit(solution)/shard_map/ppermute | solution.py:424
  186.8 5.4 %collective-permute-done.42.b = f32[16,512]{1,0:T(8,128)S(1)} collective-permute-done((f32[16,512]{1,0:T(8,128)S(1)}, f32[16,512]{1,0:T(8,128)S(1)}, u32[]{:S(2)}, u32[]{:S(2)}) %collective-permute-start.42) | collective-permute-done | bytes 32800 | tf_op jit(solution)/shard_map/ppermute | solution.py:424
  (154 shorter events, 98.9 us)
Async XLA Ops:
  2.5 11.6 %collective-permute-start = (f32[128,512]{1,0:T(8,128)S(1)}, f32[128,512]{1,0:T(8,128)S(1)}, u32[]{:S(2)}, u32[]{:S(2)}) collective-permute-start(f32[128,512]{1,0:T(8,128)S(1)} %get-tuple-element.78), channel_id=1, source_target_pairs={{0,1},{1,2},{2,3},{3,0},{4,5},{5,6},{6,7},{7,4},{8,9},{9,10},{10,1... | collective-permute-start | bytes 786440 | tf_op jit(solution)/shard_map/ppermute | solution.py:412
  4.1 10.7 %collective-permute-start.1 = (f32[128,512]{1,0:T(8,128)S(1)}, f32[128,512]{1,0:T(8,128)S(1)}, u32[]{:S(2)}, u32[]{:S(2)}) collective-permute-start(f32[128,512]{1,0:T(8,128)S(1)} %get-tuple-element.79), channel_id=1, source_target_pairs={{0,2},{1,3},{2,0},{3,1},{4,6},{5,7},{6,4},{7,5},{8,10},{9,11},{10,... | collective-permute-start | bytes 786440 | tf_op jit(solution)/shard_map/ppermute | solution.py:412
  6.8 11.4 %collective-permute-start.2 = (f32[128,512]{1,0:T(8,128)S(1)}, f32[128,512]{1,0:T(8,128)S(1)}, u32[]{:S(2)}, u32[]{:S(2)}) collective-permute-start(f32[128,512]{1,0:T(8,128)S(1)} %get-tuple-element.80), channel_id=1, source_target_pairs={{0,3},{1,0},{2,1},{3,2},{4,7},{5,4},{6,5},{7,6},{8,11},{9,8},{10,9... | collective-permute-start | bytes 786440 | tf_op jit(solution)/shard_map/ppermute | solution.py:412
  34.4 11.5 %collective-permute-start.8 = (f32[8,256]{1,0:T(8,128)S(1)}, f32[8,256]{1,0:T(8,128)S(1)}, u32[]{:S(2)}, u32[]{:S(2)}) collective-permute-start(f32[8,256]{1,0:T(8,128)S(1)} %add.30), channel_id=1, source_target_pairs={{0,8},{4,12},{8,16},{12,20},{16,24},{20,28},{1,9},{5,13},{9,17},{1... | collective-permute-start | bytes 24584 | tf_op jit(solution)/shard_map/ppermute | solution.py:417
  40.8 20.3 %collective-permute-start.10 = (f32[128,512]{1,0:T(8,128)}, f32[128,512]{1,0:T(8,128)S(1)}, u32[]{:S(2)}, u32[]{:S(2)}) collective-permute-start(f32[128,512]{1,0:T(8,128)} %get-tuple-element.94), channel_id=1, source_target_pairs={{0,1},{1,2},{2,3},{3,0},{4,5},{5,6},{6,7},{7,4},{8,9},{9,10},{10,1... | collective-permute-start | bytes 786440 | tf_op jit(solution)/shard_map/ppermute | solution.py:412
  41.2 19.9 %collective-permute-start.11 = (f32[128,512]{1,0:T(8,128)}, f32[128,512]{1,0:T(8,128)S(1)}, u32[]{:S(2)}, u32[]{:S(2)}) collective-permute-start(f32[128,512]{1,0:T(8,128)} %get-tuple-element.95), channel_id=1, source_target_pairs={{0,2},{1,3},{2,0},{3,1},{4,6},{5,7},{6,4},{7,5},{8,10},{9,11},{10,... | collective-permute-start | bytes 786440 | tf_op jit(solution)/shard_map/ppermute | solution.py:412
  43.6 18.2 %collective-permute-start.12 = (f32[128,512]{1,0:T(8,128)}, f32[128,512]{1,0:T(8,128)S(1)}, u32[]{:S(2)}, u32[]{:S(2)}) collective-permute-start(f32[128,512]{1,0:T(8,128)} %get-tuple-element.96), channel_id=1, source_target_pairs={{0,3},{1,0},{2,1},{3,2},{4,7},{5,4},{6,5},{7,6},{8,11},{9,8},{10,9... | collective-permute-start | bytes 786440 | tf_op jit(solution)/shard_map/ppermute | solution.py:412
  45.8 14.9 %collective-permute-start.9 = (f32[8,256]{1,0:T(8,128)S(1)}, f32[8,256]{1,0:T(8,128)S(1)}, u32[]{:S(2)}, u32[]{:S(2)}) collective-permute-start(f32[8,256]{1,0:T(8,128)S(1)} %get-tuple-element.154), channel_id=1, source_target_pairs={{0,16},{4,20},{8,24},{12,28},{1,17},{5,21},{9,25},{13,29},{2,18},{... | collective-permute-start | bytes 24584 | tf_op jit(solution)/shard_map/ppermute | solution.py:417
  67.1 9.1 %collective-permute-start.14 = (f32[320,128]{1,0:T(8,128)S(1)}, f32[320,128]{1,0:T(8,128)S(1)}, u32[]{:S(2)}, u32[]{:S(2)}) collective-permute-start(f32[320,128]{1,0:T(8,128)S(1)} %get-tuple-element.102), channel_id=1, source_target_pairs={{0,4},{4,0},{8,12},{12,8},{16,20},{20,16},{24,28},{28,24},{1,5},{5... | collective-permute-start | bytes 491528 | tf_op jit(solution)/shard_map/ppermute | solution.py:424
  76.1 63.7 %collective-permute-start.30 = (f32[128,1024]{1,0:T(8,128)}, f32[128,1024]{1,0:T(8,128)}, u32[]{:S(2)}, u32[]{:S(2)}) collective-permute-start(f32[128,1024]{1,0:T(8,128)} %get-tuple-element.127), channel_id=1, source_target_pairs={{0,1},{1,2},{2,3},{3,0},{4,5},{5,6},{6,7},{7,4},{8,9},{9,10},{10,1... | collective-permute-start | bytes 1572872 | tf_op jit(solution)/shard_map/ppermute | solution.py:412
  77.5 11.3 %collective-permute-start.19 = (f32[320,128]{1,0:T(8,128)S(1)}, f32[320,128]{1,0:T(8,128)S(1)}, u32[]{:S(2)}, u32[]{:S(2)}) collective-permute-start(f32[320,128]{1,0:T(8,128)S(1)} %add.35), channel_id=1, source_target_pairs={{16,0},{20,4},{24,8},{28,12},{17,1},{21,5},{25,9},{29,13},{18,2},{... | collective-permute-start | bytes 491528 | tf_op jit(solution)/shard_map/ppermute | solution.py:417
  78.8 13.5 %collective-permute-start.20 = (f32[320,128]{1,0:T(8,128)S(1)}, f32[320,128]{1,0:T(8,128)S(1)}, u32[]{:S(2)}, u32[]{:S(2)}) collective-permute-start(f32[320,128]{1,0:T(8,128)S(1)} %add.35), channel_id=1, source_target_pairs={{24,0},{28,4},{25,1},{29,5},{26,2},{30,6},{27,3},{31,7},{56,32},{6... | collective-permute-start | bytes 491528 | tf_op jit(solution)/shard_map/ppermute | solution.py:417
  80.4 12.0 %collective-permute-start.21 = (f32[320,128]{1,0:T(8,128)S(1)}, f32[320,128]{1,0:T(8,128)S(1)}, u32[]{:S(2)}, u32[]{:S(2)}) collective-permute-start(f32[320,128]{1,0:T(8,128)S(1)} %get-tuple-element.108), channel_id=1, source_target_pairs={{0,4},{4,0},{8,12},{12,8},{16,20},{20,16},{24,28},{28,24},{1,5},{5... | collective-permute-start | bytes 491528 | tf_op jit(solution)/shard_map/ppermute | solution.py:424
  85.0 56.6 %collective-permute-start.31 = (f32[128,1024]{1,0:T(8,128)}, f32[128,1024]{1,0:T(8,128)}, u32[]{:S(2)}, u32[]{:S(2)}) collective-permute-start(f32[128,1024]{1,0:T(8,128)} %get-tuple-element.128), channel_id=1, source_target_pairs={{0,2},{1,3},{2,0},{3,1},{4,6},{5,7},{6,4},{7,5},{8,10},{9,11},{10,... | collective-permute-start | bytes 1572872 | tf_op jit(solution)/shard_map/ppermute | solution.py:412
  88.8 52.8 %collective-permute-start.32 = (f32[128,1024]{1,0:T(8,128)}, f32[128,1024]{1,0:T(8,128)}, u32[]{:S(2)}, u32[]{:S(2)}) collective-permute-start(f32[128,1024]{1,0:T(8,128)} %get-tuple-element.129), channel_id=1, source_target_pairs={{0,3},{1,0},{2,1},{3,2},{4,7},{5,4},{6,5},{7,6},{8,11},{9,8},{10,9... | collective-permute-start | bytes 1572872 | tf_op jit(solution)/shard_map/ppermute | solution.py:412
  109.8 14.7 %collective-permute-start.22 = (f32[320,128]{1,0:T(8,128)S(1)}, f32[320,128]{1,0:T(8,128)S(1)}, u32[]{:S(2)}, u32[]{:S(2)}) collective-permute-start(f32[320,128]{1,0:T(8,128)S(1)} %get-tuple-element.112), channel_id=1, source_target_pairs={{0,4},{4,0},{8,12},{12,8},{16,20},{20,16},{24,28},{28,24},{1,5},{5... | collective-permute-start | bytes 491528 | tf_op jit(solution)/shard_map/ppermute | solution.py:424
  115.1 9.4 %collective-permute-start.25 = (f32[8,256]{1,0:T(8,128)S(1)}, f32[8,256]{1,0:T(8,128)S(1)}, u32[]{:S(2)}, u32[]{:S(2)}) collective-permute-start(f32[8,256]{1,0:T(8,128)S(1)} %get-tuple-element.152), channel_id=1, source_target_pairs={{16,0},{20,4},{24,8},{28,12},{17,1},{21,5},{25,9},{29,13},{18,2},{... | collective-permute-start | bytes 24584 | tf_op jit(solution)/shard_map/ppermute | solution.py:417
  139.8 9.1 %collective-permute-start.29 = (f32[512,128]{1,0:T(8,128)S(1)}, f32[512,128]{1,0:T(8,128)S(1)}, u32[]{:S(2)}, u32[]{:S(2)}) collective-permute-start(f32[512,128]{1,0:T(8,128)S(1)} %shard_map.121.g0), channel_id=1, source_target_pairs={{0,3},{1,0},{2,1},{3,2},{4,7},{5,4},{6,5},{7,6},{8,11},{9,8},{10,9... | collective-permute-start | bytes 786440 | tf_op jit(solution)/shard_map/ppermute | solution.py:412
  154.6 9.6 %collective-permute-start.34 = (f32[128,512]{1,0:T(8,128)S(1)}, f32[128,512]{1,0:T(8,128)S(1)}, u32[]{:S(2)}, u32[]{:S(2)}) collective-permute-start(f32[128,512]{1,0:T(8,128)S(1)} %get-tuple-element.132), channel_id=1, source_target_pairs={{0,64},{64,128},{128,192},{192,0},{1,65},{65,129},{129,193},{193,1... | collective-permute-start | bytes 786440 | tf_op jit(solution)/shard_map/ppermute | solution.py:412
  156.2 16.8 %collective-permute-start.38 = (f32[128,512]{1,0:T(8,128)}, f32[128,512]{1,0:T(8,128)S(1)}, u32[]{:S(2)}, u32[]{:S(2)}) collective-permute-start(f32[128,512]{1,0:T(8,128)} %get-tuple-element.143), channel_id=1, source_target_pairs={{0,128},{64,192},{128,0},{192,64},{1,129},{65,193},{129,1},{193,65... | collective-permute-start | bytes 786440 | tf_op jit(solution)/shard_map/ppermute | solution.py:412
  159.0 14.0 %collective-permute-start.39 = (f32[128,512]{1,0:T(8,128)S(1)}, f32[128,512]{1,0:T(8,128)S(1)}, u32[]{:S(2)}, u32[]{:S(2)}) collective-permute-start(f32[128,512]{1,0:T(8,128)S(1)} %get-tuple-element.144), channel_id=1, source_target_pairs={{0,192},{64,0},{128,64},{192,128},{1,193},{65,1},{129,65},{193,129... | collective-permute-start | bytes 786440 | tf_op jit(solution)/shard_map/ppermute | solution.py:412
  164.2 34.4 %collective-permute-start.35 = (f32[128,1024]{1,0:T(8,128)}, f32[128,1024]{1,0:T(8,128)S(1)}, u32[]{:S(2)}, u32[]{:S(2)}) collective-permute-start(f32[128,1024]{1,0:T(8,128)} %copy-done.21), channel_id=1, source_target_pairs={{0,1},{1,2},{2,3},{3,0},{4,5},{5,6},{6,7},{7,4},{8,9},{9,10},{10,1... | collective-permute-start | bytes 1572872 | tf_op jit(solution)/shard_map/ppermute | solution.py:412
  164.8 35.3 %collective-permute-start.36 = (f32[128,1024]{1,0:T(8,128)}, f32[128,1024]{1,0:T(8,128)S(1)}, u32[]{:S(2)}, u32[]{:S(2)}) collective-permute-start(f32[128,1024]{1,0:T(8,128)} %copy-done.20), channel_id=1, source_target_pairs={{0,2},{1,3},{2,0},{3,1},{4,6},{5,7},{6,4},{7,5},{8,10},{9,11},{10,... | collective-permute-start | bytes 1572872 | tf_op jit(solution)/shard_map/ppermute | solution.py:412
  166.3 33.8 %collective-permute-start.37 = (f32[128,1024]{1,0:T(8,128)}, f32[128,1024]{1,0:T(8,128)S(1)}, u32[]{:S(2)}, u32[]{:S(2)}) collective-permute-start(f32[128,1024]{1,0:T(8,128)} %copy-done.19), channel_id=1, source_target_pairs={{0,3},{1,0},{2,1},{3,2},{4,7},{5,4},{6,5},{7,6},{8,11},{9,8},{10,9... | collective-permute-start | bytes 1572872 | tf_op jit(solution)/shard_map/ppermute | solution.py:412
  (46 other events, 471.7 us)

commit v3 on v2

--- a/solution.py
+++ b/solution.py
@@ -66,7 +66,10 @@
     sm = pl.BlockSpec(memory_space=pltpu.SMEM)
     return pl.pallas_call(
         kernel,
-        out_shape=[jax.ShapeDtypeStruct(s, d) for s, d in outs],
+        out_shape=[
+            pltpu.HBM(s, d) if i in far_outs else jax.ShapeDtypeStruct(s, d)
+            for i, (s, d) in enumerate(outs)
+        ],
         in_specs=[
             sm if i < smem else pl.BlockSpec(memory_space=pltpu.HBM) if i in placed else vm
             for i in range(len(args))
@@ -79,7 +82,12 @@
         cost_estimate=pl.CostEstimate(
             flops=0, bytes_accessed=int(us * 3.5e6), transcendentals=0
         ),
-    )(*args)
+    )(
+        *[
+            pltpu.with_memory_space_constraint(a, pltpu.HBM) if i in placed else a
+            for i, a in enumerate(args)
+        ]
+    )
 
 
 def timed(us, *args, **kwargs):

time: 204 us -> 201 us (0.985)
  local copies, waits for them, and re-layouts: 11 us -> 3.53 us
  starting transfers between devices: 94.2 us -> 98.6 us
    unnamed x44 -> x28, local copies, waits for them, and re-layouts: 10.7 us -> 3.22 us
    ppermute x13, starting transfers between devices: 32.5 us -> 35.2 us  [shift_open(): lax.ppermute(value, axis, [(i, i + by) for i in range(n) if 0 <= i + by <...]
    ppermute x10, starting transfers between devices: 17.3 us -> 19.9 us  [swap(): return lax.ppermute(value, axis, [(i, i ^ mask) for i in range(n)])]
  transfers between devices with their start and end apart: 48 -> 48, of which waited for: 21 -> 21; matrix products, arithmetic and copies ran while one was open for 4% -> 4% of each run, Pallas kernels for 12% -> 13%
where the time goes in v3:
time: 201 us; the launch traced here: 200 us
  starting transfers between devices  98.6 us (49%)
  waiting for transfers between devices  56.6 us (28%)
  Pallas kernels  32.3 us (16%)
  matrix products  7.88 us (4%)
  local copies, waits for them, and re-layouts  3.53 us (2%)
    ppermute x24, starting transfers between devices, shift(): return lax.ppermute(value, axis, [(i, (i + by) % n) for i in range(n)])  40.2 us
    ppermute x13, starting transfers between devices, shift_open(): lax.ppermute(value, axis, [(i, i + by) for i in range(n) if 0 <= i + by <...  35.2 us
    pallas_call x21, Pallas kernels, run(): pl.pallas_call(kernel, out_shape=[pltpu.HBM(s, d) if i in far_outs else j...  32.3 us
    ppermute x13, waiting for transfers between devices, shift_open(): lax.ppermute(value, axis, [(i, i + by) for i in range(n) if 0 <= i + by <...  24.9 us
    ppermute x10, starting transfers between devices, swap(): return lax.ppermute(value, axis, [(i, i ^ mask) for i in range(n)])  19.9 us
    ppermute x24, waiting for transfers between devices, shift(): return lax.ppermute(value, axis, [(i, (i + by) % n) for i in range(n)])  18.3 us
    ppermute x10, waiting for transfers between devices, swap(): return lax.ppermute(value, axis, [(i, i ^ mask) for i in range(n)])  13.4 us
    dot_general x1, matrix products, mm_nt(): lax.dot_general(a, b, (((1,), (1,)), ((), ())), preferred_element_type=f32)  4.65 us
  transfers between devices with their start and end apart: 48, of which 21 were waited for; matrix products, arithmetic and copies ran while one was open for 4% of the time, Pallas kernels for 13%

profile of v3, /device:TPU:8, one launch (start us, length us, event | category | flops | bytes accessed | tf_op | source)
XLA Modules:
  0.0 200.1 jit_solution(16452714974589544525)
XLA Ops:
  7.4 3.2 %fusion.projected = f32[128,512]{1,0:T(8,128)S(1)} fusion(bf16[4096,512]{1,0:T(8,128)(2,1)} %param.9, bf16[1,128,4096]{2,1,0:T(8,128)(2,1)} %param.8), kind=kOutput, calls=%fused_computation.3 | convolution fusion | flops 536870912 | bytes 5505024 | tf_op jit(solution)/shard_map/dot_general | solution.py:469
  10.7 3.4 %collective-permute-start.3 = (f32[8,512]{1,0:T(8,128)S(1)}, f32[8,512]{1,0:T(8,128)S(1)}, u32[]{:S(2)}, u32[]{:S(2)}) collective-permute-start(f32[8,512]{1,0:T(8,128)S(1)} %slice.4), channel_id=1, source_target_pairs={{0,1},{1,2},{2,3},{3,4},{4,5},{5,6},{6,7},{7,8},{8,9},{9,10},{10,1... | collective-permute-start | bytes 49160 | tf_op jit(solution)/shard_map/ppermute | solution.py:470
  14.8 3.4 %collective-permute-done.2.v3 = f32[128,512]{1,0:T(8,128)S(1)} collective-permute-done((f32[128,512]{1,0:T(8,128)S(1)}, f32[128,512]{1,0:T(8,128)S(1)}, u32[]{:S(2)}, u32[]{:S(2)}) %collective-permute-start.2) | collective-permute-done | bytes 262176 | tf_op jit(solution)/shard_map/ppermute | solution.py:420
  29.0 4.0 %collective-permute-start.7 = (f32[8,256]{1,0:T(8,128)S(1)}, f32[8,256]{1,0:T(8,128)S(1)}, u32[]{:S(2)}, u32[]{:S(2)}) collective-permute-start(f32[8,256]{1,0:T(8,128)S(1)} %get-tuple-element.91), channel_id=1, source_target_pairs={{0,4},{4,8},{8,12},{12,16},{16,20},{20,24},{24,28},{1,5},{5,9},{9,... | collective-permute-start | bytes 24584 | tf_op jit(solution)/shard_map/ppermute | solution.py:425
  34.4 5.5 %collective-permute-start.8 = (f32[8,256]{1,0:T(8,128)S(1)}, f32[8,256]{1,0:T(8,128)S(1)}, u32[]{:S(2)}, u32[]{:S(2)}) collective-permute-start(f32[8,256]{1,0:T(8,128)S(1)} %add.30), channel_id=1, source_target_pairs={{0,8},{4,12},{8,16},{12,20},{16,24},{20,28},{1,9},{5,13},{9,17},{1... | collective-permute-start | bytes 24584 | tf_op jit(solution)/shard_map/ppermute | solution.py:425
  45.7 8.2 %collective-permute-start.9 = (f32[8,256]{1,0:T(8,128)S(1)}, f32[8,256]{1,0:T(8,128)S(1)}, u32[]{:S(2)}, u32[]{:S(2)}) collective-permute-start(f32[8,256]{1,0:T(8,128)S(1)} %get-tuple-element.154), channel_id=1, source_target_pairs={{0,16},{4,20},{8,24},{12,28},{1,17},{5,21},{9,25},{13,29},{2,18},{... | collective-permute-start | bytes 24584 | tf_op jit(solution)/shard_map/ppermute | solution.py:425
  53.9 4.1 %shard_map.114 = (f32[320,128]{1,0:T(8,128)S(1)}, f32[320,128]{1,0:T(8,128)S(1)}, bf16[512,512]{1,0:T(8,128)(2,1)S(1)}, f32[4,512,128]{2,1,0:T(8,128)S(1)}) custom-call(s32[1]{0:T(128)} %bitcast.1.p.use.bit, s32[1]{0:T(128)} %bitcast.y, bf16[4,512,128]{2,1,0:T(8,128)(2,1)S(1)} %get-tuple-element.87.uq, bf16[4,512,128]{2,1,0:T(8,128)(2,1)S(1)} %get-tuple-element.86.uk, ...), custom_call_target="tpu_custom_call" | custom-call | bytes 9800000 | tf_op jit(solution)/shard_map/pallas_call | solution.py:67
  59.0 3.7 %shard_map.116 = (f32[320,128]{1,0:T(8,128)S(1)}, f32[320,128]{1,0:T(8,128)S(1)}, bf16[512,512]{1,0:T(8,128)(2,1)S(1)}, f32[4,512,128]{2,1,0:T(8,128)S(1)}) custom-call(s32[1]{0:T(128)} %bitcast.1.p.use.bit, s32[1]{0:T(128)} %bitcast.y, bf16[4,512,128]{2,1,0:T(8,128)(2,1)S(1)} %get-tuple-element.87.uq, f32[4,512,128]{2,1,0:T(8,128)S(1)} %get-tuple-element.90.rs, ...), custom_call_target="tpu_custom_call" | custom-call | bytes 8400000 | tf_op jit(solution)/shard_map/pallas_call | solution.py:67
  66.7 5.2 %collective-permute-start.16 = (f32[320,128]{1,0:T(8,128)S(1)}, f32[320,128]{1,0:T(8,128)S(1)}, u32[]{:S(2)}, u32[]{:S(2)}) collective-permute-start(f32[320,128]{1,0:T(8,128)S(1)} %add.34), channel_id=1, source_target_pairs={{0,16},{4,20},{8,24},{12,28},{1,17},{5,21},{9,25},{13,29},{2,18},{... | collective-permute-start | bytes 491528 | tf_op jit(solution)/shard_map/ppermute | solution.py:425
  78.6 5.4 %collective-permute-start.21 = (f32[320,128]{1,0:T(8,128)S(1)}, f32[320,128]{1,0:T(8,128)S(1)}, u32[]{:S(2)}, u32[]{:S(2)}) collective-permute-start(f32[320,128]{1,0:T(8,128)S(1)} %get-tuple-element.108), channel_id=1, source_target_pairs={{0,4},{4,0},{8,12},{12,8},{16,20},{20,16},{24,28},{28,24},{1,5},{5... | collective-permute-start | bytes 491528 | tf_op jit(solution)/shard_map/ppermute | solution.py:432
  90.7 9.5 %shard_map.119 = (f32[4,128,512]{2,1,0:T(8,128)S(1)}, f32[512,128]{1,0:T(8,128)S(1)}, f32[512,512]{1,0:T(8,128)S(1)}, f32[512,128]{1,0:T(8,128)S(1)}, f32[8,256]{1,0:T(8,128)S(1)}) custom-call(s32[1]{0:T(128)} %bitcast.1.p.use.bit, bf16[4,512,128]{2,1,0:T(8,128)(2,1)S(1)} %get-tuple-element.87.uq, bf16[4,512,128]{2,1,0:T(8,128)(2,1)S(1)} %get-tuple-element.86.uk, ...), custom_call_target="tpu_custom_call" | custom-call | bytes 33250000 | tf_op jit(solution)/shard_map/pallas_call | solution.py:67
  101.5 5.3 %collective-permute-done.23 = f32[8,256]{1,0:T(8,128)S(1)} collective-permute-done((f32[8,256]{1,0:T(8,128)S(1)}, f32[8,256]{1,0:T(8,128)S(1)}, u32[]{:S(2)}, u32[]{:S(2)}) %collective-permute-start.23) | collective-permute-done | bytes 8224 | tf_op jit(solution)/shard_map/ppermute | solution.py:425
  110.3 3.2 %collective-permute-done.24 = f32[8,256]{1,0:T(8,128)S(1)} collective-permute-done((f32[8,256]{1,0:T(8,128)S(1)}, f32[8,256]{1,0:T(8,128)S(1)}, u32[]{:S(2)}, u32[]{:S(2)}) %collective-permute-start.24) | collective-permute-done | bytes 8224 | tf_op jit(solution)/shard_map/ppermute | solution.py:425
  114.7 8.2 %collective-permute-done.25 = f32[8,256]{1,0:T(8,128)S(1)} collective-permute-done((f32[8,256]{1,0:T(8,128)S(1)}, f32[8,256]{1,0:T(8,128)S(1)}, u32[]{:S(2)}, u32[]{:S(2)}) %collective-permute-start.25) | collective-permute-done | bytes 8224 | tf_op jit(solution)/shard_map/ppermute | solution.py:425
  122.9 4.6 %shard_map.120 = (f32[128,1024]{1,0:T(8,128)}, f32[128,1024]{1,0:T(8,128)}, f32[128,1024]{1,0:T(8,128)}, f32[128,1024]{1,0:T(8,128)}, f32[512,128]{1,0:T(8,128)S(1)}, /*index=5*/f32[8,128]{1,0:T(8,128)S(1)}) custom-call(s32[1]{0:T(128)} %bitcast.1.p.use.bit, s32[1]{0:T(128)} %bitcast.y, bf16[4,512,128]{2,1,0:T(8,128)(2,1)S(1)} %get-tuple-element.86.uk, ...), custom_call_target="tpu_custom_call" | custom-call | bytes 12250000 | tf_op jit(solution)/shard_map/pallas_call | solution.py:67
  129.0 4.0 %collective-permute-done.26.halo = f32[8,128]{1,0:T(8,128)S(1)} collective-permute-done((f32[8,128]{1,0:T(8,128)S(1)}, f32[8,128]{1,0:T(8,128)S(1)}, u32[]{:S(2)}, u32[]{:S(2)}) %collective-permute-start.26) | collective-permute-done | bytes 4128 | tf_op jit(solution)/shard_map/ppermute | solution.py:425
  148.5 2.9 %collective-permute-done.33.b = f32[512,512]{1,0:T(8,128)S(1)} collective-permute-done((f32[512,512]{1,0:T(8,128)}, f32[512,512]{1,0:T(8,128)S(1)}, u32[]{:S(2)}, u32[]{:S(2)}) %collective-permute-start.33) | collective-permute-done | bytes 1048608 | tf_op jit(solution)/shard_map/ppermute | solution.py:432
  153.2 2.8 %collective-permute-start.38 = (f32[128,512]{1,0:T(8,128)S(1)}, f32[128,512]{1,0:T(8,128)S(1)}, u32[]{:S(2)}, u32[]{:S(2)}) collective-permute-start(f32[128,512]{1,0:T(8,128)S(1)} %get-tuple-element.143), channel_id=1, source_target_pairs={{0,128},{64,192},{128,0},{192,64},{1,129},{65,193},{129,1},{193,65... | collective-permute-start | bytes 786440 | tf_op jit(solution)/shard_map/ppermute | solution.py:420
  157.4 3.7 %collective-permute-done.34.refs_1_ = f32[128,512]{1,0:T(8,128)S(1)} collective-permute-done((f32[128,512]{1,0:T(8,128)S(1)}, f32[128,512]{1,0:T(8,128)S(1)}, u32[]{:S(2)}, u32[]{:S(2)}) %collective-permute-start.34) | collective-permute-done | bytes 262176 | tf_op jit(solution)/shard_map/ppermute | solution.py:420
  165.5 4.7 %convolution_convert_fusion = bf16[128,4096]{1,0:T(8,128)(2,1)} fusion(bf16[128,512]{0,1:T(8,128)(2,1)S(1)} %bitcast.29, bf16[4096,512]{1,0:T(8,128)(2,1)} %param.9), kind=kOutput, calls=%fused_computation | convolution fusion | flops 537395200 | bytes 5373952 | tf_op jit(solution)/shard_map/dot_general | solution.py:57
  172.9 2.9 %collective-permute-done.40.refs_1_ = f32[64,512]{1,0:T(8,128)S(1)} collective-permute-done((f32[64,512]{1,0:T(8,128)S(1)}, f32[64,512]{1,0:T(8,128)S(1)}, u32[]{:S(2)}, u32[]{:S(2)}) %collective-permute-start.40) | collective-permute-done | bytes 131104 | tf_op jit(solution)/shard_map/ppermute | solution.py:432
  175.9 3.7 %collective-permute-start.41 = (f32[32,512]{1,0:T(8,128)S(1)}, f32[32,512]{1,0:T(8,128)S(1)}, u32[]{:S(2)}, u32[]{:S(2)}) collective-permute-start(f32[32,512]{1,0:T(8,128)S(1)} %get-tuple-element.148), channel_id=1, source_target_pairs={{0,8},{4,12},{8,0},{12,4},{16,24},{20,28},{24,16},{28,20},{1,9},{5... | collective-permute-start | bytes 196616 | tf_op jit(solution)/shard_map/ppermute | solution.py:432
  181.8 3.8 %collective-permute-start.42 = (f32[16,512]{1,0:T(8,128)S(1)}, f32[16,512]{1,0:T(8,128)S(1)}, u32[]{:S(2)}, u32[]{:S(2)}) collective-permute-start(f32[16,512]{1,0:T(8,128)S(1)} %get-tuple-element.150), channel_id=1, source_target_pairs={{0,16},{4,20},{8,24},{12,28},{16,0},{20,4},{24,8},{28,12},{1,17},{... | collective-permute-start | bytes 98312 | tf_op jit(solution)/shard_map/ppermute | solution.py:432
  185.6 4.1 %collective-permute-done.42.b = f32[16,512]{1,0:T(8,128)S(1)} collective-permute-done((f32[16,512]{1,0:T(8,128)S(1)}, f32[16,512]{1,0:T(8,128)S(1)}, u32[]{:S(2)}, u32[]{:S(2)}) %collective-permute-start.42) | collective-permute-done | bytes 32800 | tf_op jit(solution)/shard_map/ppermute | solution.py:432
  (138 shorter events, 89.5 us)
Async XLA Ops:
  2.5 11.6 %collective-permute-start = (f32[128,512]{1,0:T(8,128)S(1)}, f32[128,512]{1,0:T(8,128)S(1)}, u32[]{:S(2)}, u32[]{:S(2)}) collective-permute-start(f32[128,512]{1,0:T(8,128)S(1)} %get-tuple-element.78), channel_id=1, source_target_pairs={{0,1},{1,2},{2,3},{3,0},{4,5},{5,6},{6,7},{7,4},{8,9},{9,10},{10,1... | collective-permute-start | bytes 786440 | tf_op jit(solution)/shard_map/ppermute | solution.py:420
  4.1 10.7 %collective-permute-start.1 = (f32[128,512]{1,0:T(8,128)S(1)}, f32[128,512]{1,0:T(8,128)S(1)}, u32[]{:S(2)}, u32[]{:S(2)}) collective-permute-start(f32[128,512]{1,0:T(8,128)S(1)} %get-tuple-element.79), channel_id=1, source_target_pairs={{0,2},{1,3},{2,0},{3,1},{4,6},{5,7},{6,4},{7,5},{8,10},{9,11},{10,... | collective-permute-start | bytes 786440 | tf_op jit(solution)/shard_map/ppermute | solution.py:420
  6.8 11.4 %collective-permute-start.2 = (f32[128,512]{1,0:T(8,128)S(1)}, f32[128,512]{1,0:T(8,128)S(1)}, u32[]{:S(2)}, u32[]{:S(2)}) collective-permute-start(f32[128,512]{1,0:T(8,128)S(1)} %get-tuple-element.80), channel_id=1, source_target_pairs={{0,3},{1,0},{2,1},{3,2},{4,7},{5,4},{6,5},{7,6},{8,11},{9,8},{10,9... | collective-permute-start | bytes 786440 | tf_op jit(solution)/shard_map/ppermute | solution.py:420
  34.4 11.4 %collective-permute-start.8 = (f32[8,256]{1,0:T(8,128)S(1)}, f32[8,256]{1,0:T(8,128)S(1)}, u32[]{:S(2)}, u32[]{:S(2)}) collective-permute-start(f32[8,256]{1,0:T(8,128)S(1)} %add.30), channel_id=1, source_target_pairs={{0,8},{4,12},{8,16},{12,20},{16,24},{20,28},{1,9},{5,13},{9,17},{1... | collective-permute-start | bytes 24584 | tf_op jit(solution)/shard_map/ppermute | solution.py:425
  40.7 17.6 %collective-permute-start.10 = (f32[128,512]{1,0:T(8,128)S(1)}, f32[128,512]{1,0:T(8,128)S(1)}, u32[]{:S(2)}, u32[]{:S(2)}) collective-permute-start(f32[128,512]{1,0:T(8,128)S(1)} %get-tuple-element.94), channel_id=1, source_target_pairs={{0,1},{1,2},{2,3},{3,0},{4,5},{5,6},{6,7},{7,4},{8,9},{9,10},{10,1... | collective-permute-start | bytes 786440 | tf_op jit(solution)/shard_map/ppermute | solution.py:420
  41.1 17.2 %collective-permute-start.11 = (f32[128,512]{1,0:T(8,128)S(1)}, f32[128,512]{1,0:T(8,128)}, u32[]{:S(2)}, u32[]{:S(2)}) collective-permute-start(f32[128,512]{1,0:T(8,128)S(1)} %get-tuple-element.95), channel_id=1, source_target_pairs={{0,2},{1,3},{2,0},{3,1},{4,6},{5,7},{6,4},{7,5},{8,10},{9,11},{10,... | collective-permute-start | bytes 786440 | tf_op jit(solution)/shard_map/ppermute | solution.py:420
  43.5 14.8 %collective-permute-start.12 = (f32[128,512]{1,0:T(8,128)S(1)}, f32[128,512]{1,0:T(8,128)}, u32[]{:S(2)}, u32[]{:S(2)}) collective-permute-start(f32[128,512]{1,0:T(8,128)S(1)} %get-tuple-element.96), channel_id=1, source_target_pairs={{0,3},{1,0},{2,1},{3,2},{4,7},{5,4},{6,5},{7,6},{8,11},{9,8},{10,9... | collective-permute-start | bytes 786440 | tf_op jit(solution)/shard_map/ppermute | solution.py:420
  45.7 12.3 %collective-permute-start.9 = (f32[8,256]{1,0:T(8,128)S(1)}, f32[8,256]{1,0:T(8,128)S(1)}, u32[]{:S(2)}, u32[]{:S(2)}) collective-permute-start(f32[8,256]{1,0:T(8,128)S(1)} %get-tuple-element.154), channel_id=1, source_target_pairs={{0,16},{4,20},{8,24},{12,28},{1,17},{5,21},{9,25},{13,29},{2,18},{... | collective-permute-start | bytes 24584 | tf_op jit(solution)/shard_map/ppermute | solution.py:425
  62.7 11.8 %collective-permute-start.14 = (f32[320,128]{1,0:T(8,128)S(1)}, f32[320,128]{1,0:T(8,128)S(1)}, u32[]{:S(2)}, u32[]{:S(2)}) collective-permute-start(f32[320,128]{1,0:T(8,128)S(1)} %get-tuple-element.102), channel_id=1, source_target_pairs={{0,4},{4,0},{8,12},{12,8},{16,20},{20,16},{24,28},{28,24},{1,5},{5... | collective-permute-start | bytes 491528 | tf_op jit(solution)/shard_map/ppermute | solution.py:432
  64.7 11.2 %collective-permute-start.15 = (f32[320,128]{1,0:T(8,128)S(1)}, f32[320,128]{1,0:T(8,128)S(1)}, u32[]{:S(2)}, u32[]{:S(2)}) collective-permute-start(f32[320,128]{1,0:T(8,128)S(1)} %add.34), channel_id=1, source_target_pairs={{0,8},{4,12},{8,16},{12,20},{16,24},{20,28},{1,9},{5,13},{9,17},{1... | collective-permute-start | bytes 491528 | tf_op jit(solution)/shard_map/ppermute | solution.py:425
  66.7 10.6 %collective-permute-start.16 = (f32[320,128]{1,0:T(8,128)S(1)}, f32[320,128]{1,0:T(8,128)S(1)}, u32[]{:S(2)}, u32[]{:S(2)}) collective-permute-start(f32[320,128]{1,0:T(8,128)S(1)} %add.34), channel_id=1, source_target_pairs={{0,16},{4,20},{8,24},{12,28},{1,17},{5,21},{9,25},{13,29},{2,18},{... | collective-permute-start | bytes 491528 | tf_op jit(solution)/shard_map/ppermute | solution.py:425
  74.6 62.9 %collective-permute-start.30 = (f32[128,1024]{1,0:T(8,128)}, f32[128,1024]{1,0:T(8,128)S(1)}, u32[]{:S(2)}, u32[]{:S(2)}) collective-permute-start(f32[128,1024]{1,0:T(8,128)} %get-tuple-element.127), channel_id=1, source_target_pairs={{0,1},{1,2},{2,3},{3,0},{4,5},{5,6},{6,7},{7,4},{8,9},{9,10},{10,1... | collective-permute-start | bytes 1572872 | tf_op jit(solution)/shard_map/ppermute | solution.py:420
  75.9 11.2 %collective-permute-start.19 = (f32[320,128]{1,0:T(8,128)S(1)}, f32[320,128]{1,0:T(8,128)S(1)}, u32[]{:S(2)}, u32[]{:S(2)}) collective-permute-start(f32[320,128]{1,0:T(8,128)S(1)} %add.35), channel_id=1, source_target_pairs={{16,0},{20,4},{24,8},{28,12},{17,1},{21,5},{25,9},{29,13},{18,2},{... | collective-permute-start | bytes 491528 | tf_op jit(solution)/shard_map/ppermute | solution.py:425
  77.2 13.4 %collective-permute-start.20 = (f32[320,128]{1,0:T(8,128)S(1)}, f32[320,128]{1,0:T(8,128)S(1)}, u32[]{:S(2)}, u32[]{:S(2)}) collective-permute-start(f32[320,128]{1,0:T(8,128)S(1)} %add.35), channel_id=1, source_target_pairs={{24,0},{28,4},{25,1},{29,5},{26,2},{30,6},{27,3},{31,7},{56,32},{6... | collective-permute-start | bytes 491528 | tf_op jit(solution)/shard_map/ppermute | solution.py:425
  78.6 12.1 %collective-permute-start.21 = (f32[320,128]{1,0:T(8,128)S(1)}, f32[320,128]{1,0:T(8,128)S(1)}, u32[]{:S(2)}, u32[]{:S(2)}) collective-permute-start(f32[320,128]{1,0:T(8,128)S(1)} %get-tuple-element.108), channel_id=1, source_target_pairs={{0,4},{4,0},{8,12},{12,8},{16,20},{20,16},{24,28},{28,24},{1,5},{5... | collective-permute-start | bytes 491528 | tf_op jit(solution)/shard_map/ppermute | solution.py:432
  84.0 55.6 %collective-permute-start.31 = (f32[128,1024]{1,0:T(8,128)}, f32[128,1024]{1,0:T(8,128)}, u32[]{:S(2)}, u32[]{:S(2)}) collective-permute-start(f32[128,1024]{1,0:T(8,128)} %get-tuple-element.128), channel_id=1, source_target_pairs={{0,2},{1,3},{2,0},{3,1},{4,6},{5,7},{6,4},{7,5},{8,10},{9,11},{10,... | collective-permute-start | bytes 1572872 | tf_op jit(solution)/shard_map/ppermute | solution.py:420
  87.1 52.5 %collective-permute-start.32 = (f32[128,1024]{1,0:T(8,128)}, f32[128,1024]{1,0:T(8,128)}, u32[]{:S(2)}, u32[]{:S(2)}) collective-permute-start(f32[128,1024]{1,0:T(8,128)} %get-tuple-element.129), channel_id=1, source_target_pairs={{0,3},{1,0},{2,1},{3,2},{4,7},{5,4},{6,5},{7,6},{8,11},{9,8},{10,9... | collective-permute-start | bytes 1572872 | tf_op jit(solution)/shard_map/ppermute | solution.py:420
  108.2 14.7 %collective-permute-start.22 = (f32[320,128]{1,0:T(8,128)S(1)}, f32[320,128]{1,0:T(8,128)S(1)}, u32[]{:S(2)}, u32[]{:S(2)}) collective-permute-start(f32[320,128]{1,0:T(8,128)S(1)} %get-tuple-element.112), channel_id=1, source_target_pairs={{0,4},{4,0},{8,12},{12,8},{16,20},{20,16},{24,28},{28,24},{1,5},{5... | collective-permute-start | bytes 491528 | tf_op jit(solution)/shard_map/ppermute | solution.py:432
  151.5 9.6 %collective-permute-start.34 = (f32[128,512]{1,0:T(8,128)S(1)}, f32[128,512]{1,0:T(8,128)S(1)}, u32[]{:S(2)}, u32[]{:S(2)}) collective-permute-start(f32[128,512]{1,0:T(8,128)S(1)} %get-tuple-element.132), channel_id=1, source_target_pairs={{0,64},{64,128},{128,192},{192,0},{1,65},{65,129},{129,193},{193,1... | collective-permute-start | bytes 786440 | tf_op jit(solution)/shard_map/ppermute | solution.py:420
  153.2 17.0 %collective-permute-start.38 = (f32[128,512]{1,0:T(8,128)S(1)}, f32[128,512]{1,0:T(8,128)S(1)}, u32[]{:S(2)}, u32[]{:S(2)}) collective-permute-start(f32[128,512]{1,0:T(8,128)S(1)} %get-tuple-element.143), channel_id=1, source_target_pairs={{0,128},{64,192},{128,0},{192,64},{1,129},{65,193},{129,1},{193,65... | collective-permute-start | bytes 786440 | tf_op jit(solution)/shard_map/ppermute | solution.py:420
  156.0 14.2 %collective-permute-start.39 = (f32[128,512]{1,0:T(8,128)S(1)}, f32[128,512]{1,0:T(8,128)S(1)}, u32[]{:S(2)}, u32[]{:S(2)}) collective-permute-start(f32[128,512]{1,0:T(8,128)S(1)} %get-tuple-element.144), channel_id=1, source_target_pairs={{0,192},{64,0},{128,64},{192,128},{1,193},{65,1},{129,65},{193,129... | collective-permute-start | bytes 786440 | tf_op jit(solution)/shard_map/ppermute | solution.py:420
  161.1 33.9 %collective-permute-start.35 = (f32[128,1024]{1,0:T(8,128)}, f32[128,1024]{1,0:T(8,128)S(1)}, u32[]{:S(2)}, u32[]{:S(2)}) collective-permute-start(f32[128,1024]{1,0:T(8,128)} %get-tuple-element.134), channel_id=1, source_target_pairs={{0,1},{1,2},{2,3},{3,0},{4,5},{5,6},{6,7},{7,4},{8,9},{9,10},{10,1... | collective-permute-start | bytes 1572872 | tf_op jit(solution)/shard_map/ppermute | solution.py:420
  161.7 34.7 %collective-permute-start.36 = (f32[128,1024]{1,0:T(8,128)}, f32[128,1024]{1,0:T(8,128)S(1)}, u32[]{:S(2)}, u32[]{:S(2)}) collective-permute-start(f32[128,1024]{1,0:T(8,128)} %get-tuple-element.135), channel_id=1, source_target_pairs={{0,2},{1,3},{2,0},{3,1},{4,6},{5,7},{6,4},{7,5},{8,10},{9,11},{10,... | collective-permute-start | bytes 1572872 | tf_op jit(solution)/shard_map/ppermute | solution.py:420
  163.5 33.0 %collective-permute-start.37 = (f32[128,1024]{1,0:T(8,128)}, f32[128,1024]{1,0:T(8,128)S(1)}, u32[]{:S(2)}, u32[]{:S(2)}) collective-permute-start(f32[128,1024]{1,0:T(8,128)} %get-tuple-element.136), channel_id=1, source_target_pairs={{0,3},{1,0},{2,1},{3,2},{4,7},{5,4},{6,5},{7,6},{8,11},{9,8},{10,9... | collective-permute-start | bytes 1572872 | tf_op jit(solution)/shard_map/ppermute | solution.py:420
  (38 other events, 500.7 us)

commit v4 on v3

--- a/solution.py
+++ b/solution.py
@@ -209,19 +209,23 @@
     p, y, uq, uk, v0, v1, v2, v3, sel_k, w, keep, send, vb, rs, scratch, buffer, sems
 ):
     copies = fetch((v0, v1, v2, v3), buffer, sems)
-    for s in range(NY):
-        copies[s].wait()
-        vb[group_lanes(turned(y, -s), T)] = buffer[s].astype(bf16)
-
-    def one(h, _):
-        rk = (features(uk[h], sel_k[...]) * w[0:1]).astype(bf16)
-        s = mm_tn(rk, vb[:, lanes(h)])
-        scratch[lax.div(h, 2), pl.ds(pl.multiple_of(lax.rem(h, 2) * E, E), E)] = s[:E]
+    def sums(h, _):
         for r in range(NY):
             rows = (r + 1) * T
             t = mm_nt(uq[h, r * T : rows], uk[h, :rows])
             t = jnp.where(causal(rows, r), 0.5 + t * t * (1 / 32), 0.0)
             rs[h, r * T : rows] = jnp.broadcast_to(jnp.sum(t, 1, keepdims=True), (T, V))
+        return 0
+
+    lax.fori_loop(0, HG, sums, 0)
+    for s in range(NY):
+        copies[s].wait()
+        vb[group_lanes(turned(y, -s), T)] = buffer[s].astype(bf16)
+
+    def one(h, _):
+        rk = (features(uk[h], sel_k[...]) * w[0:1]).astype(bf16)
+        s = mm_tn(rk, vb[:, lanes(h)])
+        scratch[lax.div(h, 2), pl.ds(pl.multiple_of(lax.rem(h, 2) * E, E), E)] = s[:E]
         return 0
 
     lax.fori_loop(0, HG, one, 0)
@@ -432,10 +436,11 @@
     return lax.ppermute(value, axis, [(i, i ^ mask) for i in range(n)])
 
 
-def totals_scan(tot, sign):
-    before = shift_open(tot, "z", sign)
-    before = before + shift_open(before + tot, "z", 2 * sign)
-    return before + shift_open(before + tot, "z", 4 * sign)
+def totals_scan(tot, sign, steps):
+    before = jnp.zeros_like(tot)
+    for d in steps:
+        before = before + shift_open(before + tot, "z", d * sign)
+    return before
 
 
 def across_pairs(keep, got, sign):
@@ -481,7 +486,7 @@
         y1, *mixed, sel_k, w, smem=1, scratch=[pltpu.VMEM((TS, 128), f32)],
     )
     c_all = swap_y(run(pack_kernel, by_head, y1, after(cotangent[0], tot), smem=1))
-    etot = totals_scan(tot, 1)
+    etot = totals_scan(tot, 1, (1, 2, 4))
     half = ((2 * E, V), f32)
     half_scratch = [
         pltpu.VMEM((2, 2 * E, V), f32), pltpu.VMEM((NY, T, wide), f32),
@@ -518,7 +523,7 @@
     )
     x_all = swap_y(lax.optimization_barrier((*x_packed, g_keep))[:NY])
     (flipped,) = timed(1.9, flip_kernel, [((NZ * T, TS), bf16)], y1, *x_all, smem=1)
-    egtot = totals_scan(gtot, -1)
+    egtot = totals_scan(gtot, -1, (4, 2, 1))
 
     *both, gm, edge = timed(
         3.5, key_kernel, [((T, 2 * wide), f32)] * NY + [square, ((8, 128), f32)],
@@ -543,12 +548,7 @@
     parts = run(
         split_x_kernel, [quarter] * NX, x.reshape(1), keep, swap(send, "core", 1), smem=1
     )
-    own_rows = jnp.transpose(
-        after(grad_own, parts[0]).reshape(T, NY, 2, 64), (0, 2, 1, 3)
-    ).reshape(T, 512)
-    grad_x = mm_nt(own_rows, qk_weight).astype(bf16)
     parts = [parts[0]] + [shift(parts[s], "x", s) for s in (1, 2, 3)]
-    parts[0] = after(parts[0], grad_x)
     both = swap_y(lax.optimization_barrier((*both, parts[1]))[:NY])
     mixed_out, grad_values = run(
         rows_kernel, [((T, H * V), bf16)] * 2, y1, *both, smem=1
@@ -559,7 +559,14 @@
         keep, send = run(
             split_z_kernel, [((n, 512), f32), ((n, 512), f32)], bit, *parts, smem=1
         )
-        parts = [keep, swap(send, "z", mask)]
+        if mask == 1:
+            own_rows = jnp.transpose(
+                after(grad_own, keep).reshape(T, NY, 2, 64), (0, 2, 1, 3)
+            ).reshape(T, 512)
+            grad_x = mm_nt(own_rows, qk_weight).astype(bf16)
+            parts = [after(keep, grad_x), swap(send, "z", mask)]
+        else:
+            parts = [keep, swap(send, "z", mask)]
     (pair_rows,) = run(
         stack_kernel, [((32, 512), f32)], core.reshape(1), *parts,
         *[swap(a, "core", 1) for a in parts], smem=1,

time: 201 us -> 201 us (level)
    ppermute x10, starting transfers between devices: 19.9 us -> 16.4 us  [swap(): return lax.ppermute(value, axis, [(i, i ^ mask) for i in range(n)])]
where the time goes in v4:
time: 201 us; the launch traced here: 199 us
  starting transfers between devices  96.6 us (48%)
  waiting for transfers between devices  57.7 us (29%)
  Pallas kernels  32.4 us (16%)
  matrix products  7.87 us (4%)
  local copies, waits for them, and re-layouts  3.53 us (2%)
    ppermute x24, starting transfers between devices, shift(): return lax.ppermute(value, axis, [(i, (i + by) % n) for i in range(n)])  41.1 us
    ppermute x13, starting transfers between devices, shift_open(): lax.ppermute(value, axis, [(i, i + by) for i in range(n) if 0 <= i + by <...  35.7 us
    pallas_call x21, Pallas kernels, run(): pl.pallas_call(kernel, out_shape=[pltpu.HBM(s, d) if i in far_outs else j...  32.4 us
    ppermute x13, waiting for transfers between devices, shift_open(): lax.ppermute(value, axis, [(i, i + by) for i in range(n) if 0 <= i + by <...  23.5 us
    ppermute x24, waiting for transfers between devices, shift(): return lax.ppermute(value, axis, [(i, (i + by) % n) for i in range(n)])  19.8 us
    ppermute x10, starting transfers between devices, swap(): return lax.ppermute(value, axis, [(i, i ^ mask) for i in range(n)])  16.4 us
    ppermute x10, waiting for transfers between devices, swap(): return lax.ppermute(value, axis, [(i, i ^ mask) for i in range(n)])  14.4 us
    dot_general x1, matrix products, mm_nt(): lax.dot_general(a, b, (((1,), (1,)), ((), ())), preferred_element_type=f32)  4.65 us
  transfers between devices with their start and end apart: 48, of which 21 were waited for; matrix products, arithmetic and copies ran while one was open for 4% of the time, Pallas kernels for 13%

profile of v4, /device:TPU:8, one launch (start us, length us, event | category | flops | bytes accessed | tf_op | source)
XLA Modules:
  0.0 199.4 jit_solution(9809725914149498600)
XLA Ops:
  7.4 3.2 %fusion.projected = f32[128,512]{1,0:T(8,128)S(1)} fusion(bf16[4096,512]{1,0:T(8,128)(2,1)} %param.9, bf16[1,128,4096]{2,1,0:T(8,128)(2,1)} %param.8), kind=kOutput, calls=%fused_computation.3 | convolution fusion | flops 536870912 | bytes 5505024 | tf_op jit(solution)/shard_map/dot_general | solution.py:474
  10.7 3.4 %collective-permute-start.3 = (f32[8,512]{1,0:T(8,128)S(1)}, f32[8,512]{1,0:T(8,128)S(1)}, u32[]{:S(2)}, u32[]{:S(2)}) collective-permute-start(f32[8,512]{1,0:T(8,128)S(1)} %slice.4), channel_id=1, source_target_pairs={{0,1},{1,2},{2,3},{3,4},{4,5},{5,6},{6,7},{7,8},{8,9},{9,10},{10,1... | collective-permute-start | bytes 49160 | tf_op jit(solution)/shard_map/ppermute | solution.py:475
  14.8 3.4 %collective-permute-done.2.v3 = f32[128,512]{1,0:T(8,128)S(1)} collective-permute-done((f32[128,512]{1,0:T(8,128)S(1)}, f32[128,512]{1,0:T(8,128)S(1)}, u32[]{:S(2)}, u32[]{:S(2)}) %collective-permute-start.2) | collective-permute-done | bytes 262176 | tf_op jit(solution)/shard_map/ppermute | solution.py:424
  22.9 2.8 %collective-permute-done.5.b2 = f32[128,128]{1,0:T(8,128)S(1)} collective-permute-done((f32[128,128]{1,0:T(8,128)S(1)}, f32[128,128]{1,0:T(8,128)S(1)}, u32[]{:S(2)}, u32[]{:S(2)}) %collective-permute-start.5) | collective-permute-done | bytes 65568 | tf_op jit(solution)/shard_map/ppermute | solution.py:424
  29.0 4.0 %collective-permute-start.7 = (f32[8,256]{1,0:T(8,128)S(1)}, f32[8,256]{1,0:T(8,128)S(1)}, u32[]{:S(2)}, u32[]{:S(2)}) collective-permute-start(f32[8,256]{1,0:T(8,128)S(1)} %get-tuple-element.91), channel_id=1, source_target_pairs={{0,4},{4,8},{8,12},{12,16},{16,20},{20,24},{24,28},{1,5},{5,9},{9,... | collective-permute-start | bytes 24584 | tf_op jit(solution)/shard_map/ppermute | solution.py:429
  34.4 5.5 %collective-permute-start.8 = (f32[8,256]{1,0:T(8,128)S(1)}, f32[8,256]{1,0:T(8,128)S(1)}, u32[]{:S(2)}, u32[]{:S(2)}) collective-permute-start(f32[8,256]{1,0:T(8,128)S(1)} %add.30), channel_id=1, source_target_pairs={{0,8},{4,12},{8,16},{12,20},{16,24},{20,28},{1,9},{5,13},{9,17},{1... | collective-permute-start | bytes 24584 | tf_op jit(solution)/shard_map/ppermute | solution.py:429
  45.7 8.2 %collective-permute-start.9 = (f32[8,256]{1,0:T(8,128)S(1)}, f32[8,256]{1,0:T(8,128)S(1)}, u32[]{:S(2)}, u32[]{:S(2)}) collective-permute-start(f32[8,256]{1,0:T(8,128)S(1)} %get-tuple-element.154), channel_id=1, source_target_pairs={{0,16},{4,20},{8,24},{12,28},{1,17},{5,21},{9,25},{13,29},{2,18},{... | collective-permute-start | bytes 24584 | tf_op jit(solution)/shard_map/ppermute | solution.py:429
  53.9 3.6 %shard_map.114 = (f32[320,128]{1,0:T(8,128)S(1)}, f32[320,128]{1,0:T(8,128)S(1)}, bf16[512,512]{1,0:T(8,128)(2,1)S(1)}, f32[4,512,128]{2,1,0:T(8,128)S(1)}) custom-call(s32[1]{0:T(128)} %bitcast.1.p.use.bit, s32[1]{0:T(128)} %bitcast.y, bf16[4,512,128]{2,1,0:T(8,128)(2,1)S(1)} %get-tuple-element.87.uq, bf16[4,512,128]{2,1,0:T(8,128)(2,1)S(1)} %get-tuple-element.86.uk, ...), custom_call_target="tpu_custom_call" | custom-call | bytes 9800000 | tf_op jit(solution)/shard_map/pallas_call | solution.py:67
  58.5 3.7 %shard_map.116 = (f32[320,128]{1,0:T(8,128)S(1)}, f32[320,128]{1,0:T(8,128)S(1)}, bf16[512,512]{1,0:T(8,128)(2,1)S(1)}, f32[4,512,128]{2,1,0:T(8,128)S(1)}) custom-call(s32[1]{0:T(128)} %bitcast.1.p.use.bit, s32[1]{0:T(128)} %bitcast.y, bf16[4,512,128]{2,1,0:T(8,128)(2,1)S(1)} %get-tuple-element.87.uq, f32[4,512,128]{2,1,0:T(8,128)S(1)} %get-tuple-element.90.rs, ...), custom_call_target="tpu_custom_call" | custom-call | bytes 8400000 | tf_op jit(solution)/shard_map/pallas_call | solution.py:67
  65.9 6.0 %collective-permute-start.16 = (f32[320,128]{1,0:T(8,128)S(1)}, f32[320,128]{1,0:T(8,128)S(1)}, u32[]{:S(2)}, u32[]{:S(2)}) collective-permute-start(f32[320,128]{1,0:T(8,128)S(1)} %add.34), channel_id=1, source_target_pairs={{0,16},{4,20},{8,24},{12,28},{1,17},{5,21},{9,25},{13,29},{2,18},{... | collective-permute-start | bytes 491528 | tf_op jit(solution)/shard_map/ppermute | solution.py:429
  78.6 5.5 %collective-permute-start.21 = (f32[320,128]{1,0:T(8,128)S(1)}, f32[320,128]{1,0:T(8,128)S(1)}, u32[]{:S(2)}, u32[]{:S(2)}) collective-permute-start(f32[320,128]{1,0:T(8,128)S(1)} %get-tuple-element.108), channel_id=1, source_target_pairs={{0,4},{4,0},{8,12},{12,8},{16,20},{20,16},{24,28},{28,24},{1,5},{5... | collective-permute-start | bytes 491528 | tf_op jit(solution)/shard_map/ppermute | solution.py:436
  90.7 9.5 %shard_map.119 = (f32[4,128,512]{2,1,0:T(8,128)S(1)}, f32[512,128]{1,0:T(8,128)S(1)}, f32[512,512]{1,0:T(8,128)S(1)}, f32[512,128]{1,0:T(8,128)S(1)}, f32[8,256]{1,0:T(8,128)S(1)}) custom-call(s32[1]{0:T(128)} %bitcast.1.p.use.bit, bf16[4,512,128]{2,1,0:T(8,128)(2,1)S(1)} %get-tuple-element.87.uq, bf16[4,512,128]{2,1,0:T(8,128)(2,1)S(1)} %get-tuple-element.86.uk, ...), custom_call_target="tpu_custom_call" | custom-call | bytes 33250000 | tf_op jit(solution)/shard_map/pallas_call | solution.py:67
  101.5 8.2 %collective-permute-done.23 = f32[8,256]{1,0:T(8,128)S(1)} collective-permute-done((f32[8,256]{1,0:T(8,128)S(1)}, f32[8,256]{1,0:T(8,128)S(1)}, u32[]{:S(2)}, u32[]{:S(2)}) %collective-permute-start.23) | collective-permute-done | bytes 8224 | tf_op jit(solution)/shard_map/ppermute | solution.py:429
  111.0 3.3 %collective-permute-start.22 = (f32[320,128]{1,0:T(8,128)S(1)}, f32[320,128]{1,0:T(8,128)S(1)}, u32[]{:S(2)}, u32[]{:S(2)}) collective-permute-start(f32[320,128]{1,0:T(8,128)S(1)} %get-tuple-element.112), channel_id=1, source_target_pairs={{0,4},{4,0},{8,12},{12,8},{16,20},{20,16},{24,28},{28,24},{1,5},{5... | collective-permute-start | bytes 491528 | tf_op jit(solution)/shard_map/ppermute | solution.py:436
  117.5 5.3 %collective-permute-done.25 = f32[8,256]{1,0:T(8,128)S(1)} collective-permute-done((f32[8,256]{1,0:T(8,128)S(1)}, f32[8,256]{1,0:T(8,128)S(1)}, u32[]{:S(2)}, u32[]{:S(2)}) %collective-permute-start.25) | collective-permute-done | bytes 8224 | tf_op jit(solution)/shard_map/ppermute | solution.py:429
  122.9 4.6 %shard_map.120 = (f32[128,1024]{1,0:T(8,128)}, f32[128,1024]{1,0:T(8,128)}, f32[128,1024]{1,0:T(8,128)}, f32[128,1024]{1,0:T(8,128)}, f32[512,128]{1,0:T(8,128)S(1)}, /*index=5*/f32[8,128]{1,0:T(8,128)S(1)}) custom-call(s32[1]{0:T(128)} %bitcast.1.p.use.bit, s32[1]{0:T(128)} %bitcast.y, bf16[4,512,128]{2,1,0:T(8,128)(2,1)S(1)} %get-tuple-element.86.uk, ...), custom_call_target="tpu_custom_call" | custom-call | bytes 12250000 | tf_op jit(solution)/shard_map/pallas_call | solution.py:67
  129.0 4.0 %collective-permute-done.26.halo = f32[8,128]{1,0:T(8,128)S(1)} collective-permute-done((f32[8,128]{1,0:T(8,128)S(1)}, f32[8,128]{1,0:T(8,128)S(1)}, u32[]{:S(2)}, u32[]{:S(2)}) %collective-permute-start.26) | collective-permute-done | bytes 4128 | tf_op jit(solution)/shard_map/ppermute | solution.py:429
  148.4 2.9 %collective-permute-done.33.b = f32[512,512]{1,0:T(8,128)S(1)} collective-permute-done((f32[512,512]{1,0:T(8,128)}, f32[512,512]{1,0:T(8,128)S(1)}, u32[]{:S(2)}, u32[]{:S(2)}) %collective-permute-start.33) | collective-permute-done | bytes 1048608 | tf_op jit(solution)/shard_map/ppermute | solution.py:436
  153.5 2.7 %collective-permute-start.38 = (f32[128,512]{1,0:T(8,128)}, f32[128,512]{1,0:T(8,128)S(1)}, u32[]{:S(2)}, u32[]{:S(2)}) collective-permute-start(f32[128,512]{1,0:T(8,128)} %get-tuple-element.140), channel_id=1, source_target_pairs={{0,128},{64,192},{128,0},{192,64},{1,129},{65,193},{129,1},{193,65... | collective-permute-start | bytes 786440 | tf_op jit(solution)/shard_map/ppermute | solution.py:424
  157.7 3.9 %collective-permute-done.34.refs_1_ = f32[128,512]{1,0:T(8,128)S(1)} collective-permute-done((f32[128,512]{1,0:T(8,128)S(1)}, f32[128,512]{1,0:T(8,128)S(1)}, u32[]{:S(2)}, u32[]{:S(2)}) %collective-permute-start.34) | collective-permute-done | bytes 262176 | tf_op jit(solution)/shard_map/ppermute | solution.py:424
  170.5 4.6 %convolution_convert_fusion = bf16[128,4096]{1,0:T(8,128)(2,1)} fusion(bf16[128,512]{0,1:T(8,128)(2,1)S(1)} %bitcast.29, bf16[4096,512]{1,0:T(8,128)(2,1)} %param.9), kind=kOutput, calls=%fused_computation | convolution fusion | flops 537395200 | bytes 5373952 | tf_op jit(solution)/shard_map/dot_general | solution.py:57
  177.6 3.3 %collective-permute-done.41.refs_1_ = f32[32,512]{1,0:T(8,128)S(1)} collective-permute-done((f32[32,512]{1,0:T(8,128)S(1)}, f32[32,512]{1,0:T(8,128)S(1)}, u32[]{:S(2)}, u32[]{:S(2)}) %collective-permute-start.41) | collective-permute-done | bytes 65568 | tf_op jit(solution)/shard_map/ppermute | solution.py:436
  181.8 7.0 %collective-permute-done.42.b = f32[16,512]{1,0:T(8,128)S(1)} collective-permute-done((f32[16,512]{1,0:T(8,128)S(1)}, f32[16,512]{1,0:T(8,128)S(1)}, u32[]{:S(2)}, u32[]{:S(2)}) %collective-permute-start.42) | collective-permute-done | bytes 32800 | tf_op jit(solution)/shard_map/ppermute | solution.py:436
  191.5 2.8 %collective-permute-start.46 = (f32[32,512]{1,0:T(8,128)S(1)}, f32[32,512]{1,0:T(8,128)S(1)}, u32[]{:S(2)}, u32[]{:S(2)}) collective-permute-start(f32[32,512]{1,0:T(8,128)S(1)} %shard_map.130.m0), channel_id=1, source_target_pairs={{0,128},{64,192},{128,0},{192,64},{1,129},{65,193},{129,1},{193,65... | collective-permute-start | bytes 196616 | tf_op jit(solution)/shard_map/ppermute | solution.py:424
  (138 shorter events, 86.8 us)
Async XLA Ops:
  2.5 11.6 %collective-permute-start = (f32[128,512]{1,0:T(8,128)S(1)}, f32[128,512]{1,0:T(8,128)S(1)}, u32[]{:S(2)}, u32[]{:S(2)}) collective-permute-start(f32[128,512]{1,0:T(8,128)S(1)} %get-tuple-element.78), channel_id=1, source_target_pairs={{0,1},{1,2},{2,3},{3,0},{4,5},{5,6},{6,7},{7,4},{8,9},{9,10},{10,1... | collective-permute-start | bytes 786440 | tf_op jit(solution)/shard_map/ppermute | solution.py:424
  4.1 10.7 %collective-permute-start.1 = (f32[128,512]{1,0:T(8,128)S(1)}, f32[128,512]{1,0:T(8,128)S(1)}, u32[]{:S(2)}, u32[]{:S(2)}) collective-permute-start(f32[128,512]{1,0:T(8,128)S(1)} %get-tuple-element.79), channel_id=1, source_target_pairs={{0,2},{1,3},{2,0},{3,1},{4,6},{5,7},{6,4},{7,5},{8,10},{9,11},{10,... | collective-permute-start | bytes 786440 | tf_op jit(solution)/shard_map/ppermute | solution.py:424
  6.8 11.4 %collective-permute-start.2 = (f32[128,512]{1,0:T(8,128)S(1)}, f32[128,512]{1,0:T(8,128)S(1)}, u32[]{:S(2)}, u32[]{:S(2)}) collective-permute-start(f32[128,512]{1,0:T(8,128)S(1)} %get-tuple-element.80), channel_id=1, source_target_pairs={{0,3},{1,0},{2,1},{3,2},{4,7},{5,4},{6,5},{7,6},{8,11},{9,8},{10,9... | collective-permute-start | bytes 786440 | tf_op jit(solution)/shard_map/ppermute | solution.py:424
  34.4 11.4 %collective-permute-start.8 = (f32[8,256]{1,0:T(8,128)S(1)}, f32[8,256]{1,0:T(8,128)S(1)}, u32[]{:S(2)}, u32[]{:S(2)}) collective-permute-start(f32[8,256]{1,0:T(8,128)S(1)} %add.30), channel_id=1, source_target_pairs={{0,8},{4,12},{8,16},{12,20},{16,24},{20,28},{1,9},{5,13},{9,17},{1... | collective-permute-start | bytes 24584 | tf_op jit(solution)/shard_map/ppermute | solution.py:429
  40.7 17.0 %collective-permute-start.10 = (f32[128,512]{1,0:T(8,128)S(1)}, f32[128,512]{1,0:T(8,128)S(1)}, u32[]{:S(2)}, u32[]{:S(2)}) collective-permute-start(f32[128,512]{1,0:T(8,128)S(1)} %get-tuple-element.94), channel_id=1, source_target_pairs={{0,1},{1,2},{2,3},{3,0},{4,5},{5,6},{6,7},{7,4},{8,9},{9,10},{10,1... | collective-permute-start | bytes 786440 | tf_op jit(solution)/shard_map/ppermute | solution.py:424
  41.1 16.7 %collective-permute-start.11 = (f32[128,512]{1,0:T(8,128)S(1)}, f32[128,512]{1,0:T(8,128)}, u32[]{:S(2)}, u32[]{:S(2)}) collective-permute-start(f32[128,512]{1,0:T(8,128)S(1)} %get-tuple-element.95), channel_id=1, source_target_pairs={{0,2},{1,3},{2,0},{3,1},{4,6},{5,7},{6,4},{7,5},{8,10},{9,11},{10,... | collective-permute-start | bytes 786440 | tf_op jit(solution)/shard_map/ppermute | solution.py:424
  43.5 14.3 %collective-permute-start.12 = (f32[128,512]{1,0:T(8,128)S(1)}, f32[128,512]{1,0:T(8,128)}, u32[]{:S(2)}, u32[]{:S(2)}) collective-permute-start(f32[128,512]{1,0:T(8,128)S(1)} %get-tuple-element.96), channel_id=1, source_target_pairs={{0,3},{1,0},{2,1},{3,2},{4,7},{5,4},{6,5},{7,6},{8,11},{9,8},{10,9... | collective-permute-start | bytes 786440 | tf_op jit(solution)/shard_map/ppermute | solution.py:424
  45.7 11.8 %collective-permute-start.9 = (f32[8,256]{1,0:T(8,128)S(1)}, f32[8,256]{1,0:T(8,128)S(1)}, u32[]{:S(2)}, u32[]{:S(2)}) collective-permute-start(f32[8,256]{1,0:T(8,128)S(1)} %get-tuple-element.154), channel_id=1, source_target_pairs={{0,16},{4,20},{8,24},{12,28},{1,17},{5,21},{9,25},{13,29},{2,18},{... | collective-permute-start | bytes 24584 | tf_op jit(solution)/shard_map/ppermute | solution.py:429
  62.2 12.4 %collective-permute-start.14 = (f32[320,128]{1,0:T(8,128)S(1)}, f32[320,128]{1,0:T(8,128)S(1)}, u32[]{:S(2)}, u32[]{:S(2)}) collective-permute-start(f32[320,128]{1,0:T(8,128)S(1)} %get-tuple-element.102), channel_id=1, source_target_pairs={{0,4},{4,0},{8,12},{12,8},{16,20},{20,16},{24,28},{28,24},{1,5},{5... | collective-permute-start | bytes 491528 | tf_op jit(solution)/shard_map/ppermute | solution.py:436
  64.2 11.7 %collective-permute-start.15 = (f32[320,128]{1,0:T(8,128)S(1)}, f32[320,128]{1,0:T(8,128)S(1)}, u32[]{:S(2)}, u32[]{:S(2)}) collective-permute-start(f32[320,128]{1,0:T(8,128)S(1)} %add.34), channel_id=1, source_target_pairs={{0,8},{4,12},{8,16},{12,20},{16,24},{20,28},{1,9},{5,13},{9,17},{1... | collective-permute-start | bytes 491528 | tf_op jit(solution)/shard_map/ppermute | solution.py:429
  65.9 11.3 %collective-permute-start.16 = (f32[320,128]{1,0:T(8,128)S(1)}, f32[320,128]{1,0:T(8,128)S(1)}, u32[]{:S(2)}, u32[]{:S(2)}) collective-permute-start(f32[320,128]{1,0:T(8,128)S(1)} %add.34), channel_id=1, source_target_pairs={{0,16},{4,20},{8,24},{12,28},{1,17},{5,21},{9,25},{13,29},{2,18},{... | collective-permute-start | bytes 491528 | tf_op jit(solution)/shard_map/ppermute | solution.py:429
  74.6 63.6 %collective-permute-start.30 = (f32[128,1024]{1,0:T(8,128)}, f32[128,1024]{1,0:T(8,128)S(1)}, u32[]{:S(2)}, u32[]{:S(2)}) collective-permute-start(f32[128,1024]{1,0:T(8,128)} %get-tuple-element.127), channel_id=1, source_target_pairs={{0,1},{1,2},{2,3},{3,0},{4,5},{5,6},{6,7},{7,4},{8,9},{9,10},{10,1... | collective-permute-start | bytes 1572872 | tf_op jit(solution)/shard_map/ppermute | solution.py:424
  75.9 11.2 %collective-permute-start.19 = (f32[320,128]{1,0:T(8,128)S(1)}, f32[320,128]{1,0:T(8,128)S(1)}, u32[]{:S(2)}, u32[]{:S(2)}) collective-permute-start(f32[320,128]{1,0:T(8,128)S(1)} %add.35), channel_id=1, source_target_pairs={{16,0},{20,4},{24,8},{28,12},{17,1},{21,5},{25,9},{29,13},{18,2},{... | collective-permute-start | bytes 491528 | tf_op jit(solution)/shard_map/ppermute | solution.py:429
  77.2 13.4 %collective-permute-start.20 = (f32[320,128]{1,0:T(8,128)S(1)}, f32[320,128]{1,0:T(8,128)S(1)}, u32[]{:S(2)}, u32[]{:S(2)}) collective-permute-start(f32[320,128]{1,0:T(8,128)S(1)} %add.35), channel_id=1, source_target_pairs={{24,0},{28,4},{25,1},{29,5},{26,2},{30,6},{27,3},{31,7},{56,32},{6... | collective-permute-start | bytes 491528 | tf_op jit(solution)/shard_map/ppermute | solution.py:429
  78.6 12.1 %collective-permute-start.21 = (f32[320,128]{1,0:T(8,128)S(1)}, f32[320,128]{1,0:T(8,128)S(1)}, u32[]{:S(2)}, u32[]{:S(2)}) collective-permute-start(f32[320,128]{1,0:T(8,128)S(1)} %get-tuple-element.108), channel_id=1, source_target_pairs={{0,4},{4,0},{8,12},{12,8},{16,20},{20,16},{24,28},{28,24},{1,5},{5... | collective-permute-start | bytes 491528 | tf_op jit(solution)/shard_map/ppermute | solution.py:436
  84.1 55.6 %collective-permute-start.31 = (f32[128,1024]{1,0:T(8,128)}, f32[128,1024]{1,0:T(8,128)}, u32[]{:S(2)}, u32[]{:S(2)}) collective-permute-start(f32[128,1024]{1,0:T(8,128)} %get-tuple-element.128), channel_id=1, source_target_pairs={{0,2},{1,3},{2,0},{3,1},{4,6},{5,7},{6,4},{7,5},{8,10},{9,11},{10,... | collective-permute-start | bytes 1572872 | tf_op jit(solution)/shard_map/ppermute | solution.py:424
  87.1 52.5 %collective-permute-start.32 = (f32[128,1024]{1,0:T(8,128)}, f32[128,1024]{1,0:T(8,128)}, u32[]{:S(2)}, u32[]{:S(2)}) collective-permute-start(f32[128,1024]{1,0:T(8,128)} %get-tuple-element.129), channel_id=1, source_target_pairs={{0,3},{1,0},{2,1},{3,2},{4,7},{5,4},{6,5},{7,6},{8,11},{9,8},{10,9... | collective-permute-start | bytes 1572872 | tf_op jit(solution)/shard_map/ppermute | solution.py:424
  111.0 11.9 %collective-permute-start.22 = (f32[320,128]{1,0:T(8,128)S(1)}, f32[320,128]{1,0:T(8,128)S(1)}, u32[]{:S(2)}, u32[]{:S(2)}) collective-permute-start(f32[320,128]{1,0:T(8,128)S(1)} %get-tuple-element.112), channel_id=1, source_target_pairs={{0,4},{4,0},{8,12},{12,8},{16,20},{20,16},{24,28},{28,24},{1,5},{5... | collective-permute-start | bytes 491528 | tf_op jit(solution)/shard_map/ppermute | solution.py:436
  152.1 9.6 %collective-permute-start.34 = (f32[128,512]{1,0:T(8,128)S(1)}, f32[128,512]{1,0:T(8,128)S(1)}, u32[]{:S(2)}, u32[]{:S(2)}) collective-permute-start(f32[128,512]{1,0:T(8,128)S(1)} %get-tuple-element.132), channel_id=1, source_target_pairs={{0,64},{64,128},{128,192},{192,0},{1,65},{65,129},{129,193},{193,1... | collective-permute-start | bytes 786440 | tf_op jit(solution)/shard_map/ppermute | solution.py:424
  153.5 14.7 %collective-permute-start.38 = (f32[128,512]{1,0:T(8,128)}, f32[128,512]{1,0:T(8,128)S(1)}, u32[]{:S(2)}, u32[]{:S(2)}) collective-permute-start(f32[128,512]{1,0:T(8,128)} %get-tuple-element.140), channel_id=1, source_target_pairs={{0,128},{64,192},{128,0},{192,64},{1,129},{65,193},{129,1},{193,65... | collective-permute-start | bytes 786440 | tf_op jit(solution)/shard_map/ppermute | solution.py:424
  156.3 11.9 %collective-permute-start.39 = (f32[128,512]{1,0:T(8,128)S(1)}, f32[128,512]{1,0:T(8,128)S(1)}, u32[]{:S(2)}, u32[]{:S(2)}) collective-permute-start(f32[128,512]{1,0:T(8,128)S(1)} %get-tuple-element.141), channel_id=1, source_target_pairs={{0,192},{64,0},{128,64},{192,128},{1,193},{65,1},{129,65},{193,129... | collective-permute-start | bytes 786440 | tf_op jit(solution)/shard_map/ppermute | solution.py:424
  161.6 32.7 %collective-permute-start.35 = (f32[128,1024]{1,0:T(8,128)}, f32[128,1024]{1,0:T(8,128)S(1)}, u32[]{:S(2)}, u32[]{:S(2)}) collective-permute-start(f32[128,1024]{1,0:T(8,128)} %get-tuple-element.134), channel_id=1, source_target_pairs={{0,1},{1,2},{2,3},{3,0},{4,5},{5,6},{6,7},{7,4},{8,9},{9,10},{10,1... | collective-permute-start | bytes 1572872 | tf_op jit(solution)/shard_map/ppermute | solution.py:424
  162.2 33.4 %collective-permute-start.36 = (f32[128,1024]{1,0:T(8,128)}, f32[128,1024]{1,0:T(8,128)S(1)}, u32[]{:S(2)}, u32[]{:S(2)}) collective-permute-start(f32[128,1024]{1,0:T(8,128)} %get-tuple-element.135), channel_id=1, source_target_pairs={{0,2},{1,3},{2,0},{3,1},{4,6},{5,7},{6,4},{7,5},{8,10},{9,11},{10,... | collective-permute-start | bytes 1572872 | tf_op jit(solution)/shard_map/ppermute | solution.py:424
  164.8 30.8 %collective-permute-start.37 = (f32[128,1024]{1,0:T(8,128)}, f32[128,1024]{1,0:T(8,128)S(1)}, u32[]{:S(2)}, u32[]{:S(2)}) collective-permute-start(f32[128,1024]{1,0:T(8,128)} %get-tuple-element.136), channel_id=1, source_target_pairs={{0,3},{1,0},{2,1},{3,2},{4,7},{5,4},{6,5},{7,6},{8,11},{9,8},{10,9... | collective-permute-start | bytes 1572872 | tf_op jit(solution)/shard_map/ppermute | solution.py:424
  (38 other events, 502.0 us)
